TPU v7x, 32 devices: a whole 2x2x4 slice. The times are simulated.
32 devices in a mesh: mesh: 4 (over z), modes: 8 (over y, x, core).
Axes of the slice: x: 2, y: 2, z: 4, core: 2. Of those that a mesh axis runs over, the one named last changes fastest.
Arguments:
- velocity: float32 [3, 128, 81, 512], P(None, 'modes', None, 'mesh'), may hold values from -2 to 2
- metrics: float32 [4, 512], P(None, 'mesh'), as said below
- connect: int32 [512, 4], P('mesh'), may hold values from -1 to 511, as said below
- send_list: int32 [8, 64], P('mesh'), may hold values from 0 to 127, as said below
- recv_slot: int32 [512, 2], P('mesh'), may hold values from -1 to 63, as said below
Outputs:
- new_velocity: float32 [3, 128, 81, 512], P(None, 'modes', None, 'mesh')
- advection: float32 [3, 128, 81, 512], P(None, 'modes', None, 'mesh')
Inputs may be any that keep to these rules, and one draw needn't show every extreme that they name: Elements p * 128 to (p + 1) * 128 - 1 form partition p. connect[e, k] is the element across edge k of element e (0 bottom, 1 right, 2 top, 3 left), -1 where that edge is on the cylinder wall or the outer boundary; where recv_slot of that edge is -1 the neighbour lies in e's own partition, and neighbours across edges 1 and 3 always do. Row 2p (row 2p + 1) of send_list names, for each of the 64 edges shared with partition p - 1 (p + 1), the local index within partition p of the element whose bottom (top) edge it is; each row names 64 different elements. recv_slot[e, 0] is the column c such that the bottom neighbour of e is named by send_list[2p - 1, c] of partition p - 1, and -1 where that neighbour is in e's own partition or absent; recv_slot[e, 1] likewise for the top neighbour with send_list[2p + 2, c] of partition p + 1. `metrics`: rows 0 and 3 are positive stretches, rows 1 and 2 smaller shears.
All inputs are finite; a program needn't handle non-finite values.
Results may differ from a plain program's by a relative error of at most 0.0001.
Values sent between devices are 32-bit elements; how exact they have to be, the bound alone decides.
A program may use at most 192 MiB of HBM per device.

v0:
```python
import jax
import jax.numpy as jnp
import numpy as np
from jax import lax
from jax.sharding import PartitionSpec as P

COEF = 128
ITERS = 2


highest = lax.Precision.HIGHEST
helm_shift = 4.0
penalty_weight = 200.0
spectral_bound = 400.0
relaxation = 0.8
time_step = 0.02
wave_scale = 0.125
gll_interior = [
    -0.8997579954114602,
    -0.6771862795107377,
    -0.3631174638261782,
    0.0,
    0.3631174638261782,
    0.6771862795107377,
    0.8997579954114602,
]


def shifted(block, axis, distance):
    devices = range(lax.axis_size(axis))
    route = [(i - distance, i) for i in devices if i - distance in devices]
    return lax.ppermute(block, axis, route)


def legendre_value(point, degree):
    previous = 1.0
    current = point
    for order_index in range(1, degree):
        following = ((2 * order_index + 1) * point * current - order_index * previous) / (
            order_index + 1
        )
        previous = current
        current = following
    return current


def spectral_tables(coef_count):
    poly_order = 8
    node_count = poly_order + 1
    points = np.array([-1.0] + gll_interior + [1.0])
    values = np.array([legendre_value(points[node], poly_order) for node in range(node_count)])
    derivative = np.zeros((node_count, node_count))
    for row_index in range(node_count):
        for col_index in range(node_count):
            if row_index != col_index:
                derivative[row_index, col_index] = values[row_index] / (
                    values[col_index] * (points[row_index] - points[col_index])
                )
    derivative[0, 0] = -poly_order * (poly_order + 1) / 4.0
    derivative[poly_order, poly_order] = poly_order * (poly_order + 1) / 4.0
    identity = np.eye(node_count)
    along_r = np.kron(identity, derivative)
    along_s = np.kron(derivative, identity)
    second = np.stack([along_r @ along_r, along_r @ along_s, along_s @ along_s])
    line_nodes = np.arange(node_count)
    edge_nodes = np.stack(
        [
            line_nodes,
            line_nodes * node_count + poly_order,
            poly_order * node_count + line_nodes,
            line_nodes * node_count,
        ]
    )
    scatter_edge = np.zeros((node_count * node_count, 4 * node_count))
    for edge_index in range(4):
        scatter_edge[edge_nodes[edge_index], edge_index * node_count + line_nodes] = 1.0
    planes = np.arange(coef_count) * 2.0 * np.pi / coef_count
    half_count = coef_count // 2
    wavenumber = np.zeros(coef_count)
    basis = np.zeros((coef_count, coef_count))
    z_derivative = np.zeros((coef_count, coef_count))
    basis[:, 0] = 1.0
    basis[:, 1] = np.cos(half_count * planes)
    wavenumber[1] = half_count
    for mode_number in range(1, half_count):
        basis[:, 2 * mode_number] = np.cos(mode_number * planes)
        basis[:, 2 * mode_number + 1] = np.sin(mode_number * planes)
        wavenumber[2 * mode_number] = mode_number
        wavenumber[2 * mode_number + 1] = mode_number
        z_derivative[2 * mode_number, 2 * mode_number + 1] = wave_scale * mode_number
        z_derivative[2 * mode_number + 1, 2 * mode_number] = -wave_scale * mode_number
    norms = np.full(coef_count, coef_count / 2.0)
    norms[0] = coef_count
    norms[1] = coef_count
    inverse = basis.T / norms[:, None]
    shifts = helm_shift + (wave_scale * wavenumber) ** 2
    plane_derivative = basis @ z_derivative @ inverse
    float_tables = [
        jnp.asarray(table, dtype=jnp.float32)
        for table in (
            along_r,
            along_s,
            second,
            scatter_edge,
            basis,
            inverse,
            z_derivative,
            shifts,
            plane_derivative,
        )
    ]
    return (float_tables, edge_nodes)


def element_factors(metrics):
    return jnp.stack(
        [
            metrics[0] * metrics[0] + metrics[1] * metrics[1],
            2.0 * (metrics[0] * metrics[2] + metrics[1] * metrics[3]),
            metrics[2] * metrics[2] + metrics[3] * metrics[3],
        ]
    )


def laplacian(field, factors, second):
    total = factors[0] * jnp.einsum("qr,fcre->fcqe", second[0], field, precision=highest)
    total = total + factors[1] * jnp.einsum("qr,fcre->fcqe", second[1], field, precision=highest)
    total = total + factors[2] * jnp.einsum("qr,fcre->fcqe", second[2], field, precision=highest)
    return total


def body(velocity, metrics, connect, send_list, recv_slot):
    float_tables, edge_nodes = spectral_tables(COEF)
    (
        along_r,
        along_s,
        second,
        scatter_edge,
        basis,
        inverse,
        z_derivative,
        shifts,
        plane_derivative,
    ) = float_tables
    mode_count = lax.axis_size("modes")
    mode_index = lax.axis_index("modes")
    mesh_index = lax.axis_index("mesh")
    local_coef = velocity.shape[1]
    element_count = velocity.shape[3]
    coef_start = mode_index * local_coef
    shifts_here = lax.dynamic_slice_in_dim(shifts, coef_start, local_coef)
    basis_view = basis.reshape(COEF, mode_count, local_coef)
    inverse_view = inverse.reshape(mode_count, local_coef, COEF)
    grad_r = jnp.einsum("qr,fcre->fcqe", along_r, velocity, precision=highest)
    grad_s = jnp.einsum("qr,fcre->fcqe", along_s, velocity, precision=highest)
    grad_x = metrics[0] * grad_r + metrics[2] * grad_s
    grad_y = metrics[1] * grad_r + metrics[3] * grad_s
    z_local = lax.dynamic_slice(z_derivative, (coef_start, coef_start), (local_coef, local_coef))
    grad_z = jnp.einsum("cd,fdqe->fcqe", z_local, velocity, precision=highest)
    stacked = jnp.concatenate([velocity, grad_x, grad_y, grad_z], axis=0).reshape(
        12, local_coef, 81 * element_count
    )
    moved = lax.all_to_all(stacked, "modes", split_axis=2, concat_axis=2, tiled=True)
    point_count = 81 * element_count // mode_count
    physical = jnp.einsum(
        "psc,fcsn->fpn",
        basis_view,
        moved.reshape(12, local_coef, mode_count, point_count),
        precision=highest,
    )
    term = physical[0] * physical[3:6] + physical[1] * physical[6:9] + physical[2] * physical[9:12]
    spectral = jnp.einsum("scp,fpn->fcsn", inverse_view, term, precision=highest).reshape(
        3, local_coef, mode_count * point_count
    )
    advection = lax.all_to_all(spectral, "modes", split_axis=2, concat_axis=2, tiled=True).reshape(
        3, local_coef, 81, element_count
    )
    factors = element_factors(metrics)
    precond = (
        shifts_here[:, None] + spectral_bound * (factors[0] + factors[2])[None, :] + penalty_weight
    )
    has_local = (connect >= 0).astype(jnp.float32)
    picks = jnp.clip(connect - mesh_index * element_count, 0, element_count - 1)
    width_cols = send_list.shape[1]
    lower_cols = recv_slot[:, 0]
    upper_cols = recv_slot[:, 1]
    lower_picks = jnp.clip(lower_cols, 0, width_cols - 1)
    upper_picks = jnp.clip(upper_cols, 0, width_cols - 1)
    opposite = [2, 3, 0, 1]

    def operator(field):
        traces = field[:, :, edge_nodes, :]
        down_buffer = jnp.take(traces[:, :, 0], send_list[0], axis=-1)
        up_buffer = jnp.take(traces[:, :, 2], send_list[1], axis=-1)
        from_lower = shifted(up_buffer, "mesh", 1)
        from_upper = shifted(down_buffer, "mesh", -1)
        nearby = []
        for edge_index in range(4):
            nearby.append(
                jnp.take(traces[:, :, opposite[edge_index]], picks[:, edge_index], axis=-1)
                * has_local[:, edge_index]
            )
        nearby[0] = jnp.where(
            lower_cols >= 0, jnp.take(from_lower, lower_picks, axis=-1), nearby[0]
        )
        nearby[2] = jnp.where(
            upper_cols >= 0, jnp.take(from_upper, upper_picks, axis=-1), nearby[2]
        )
        neighbours = jnp.stack(nearby, axis=2)
        differences = (traces - neighbours).reshape(
            field.shape[0], field.shape[1], 36, field.shape[3]
        )
        penalty = jnp.einsum("qt,fcte->fcqe", scatter_edge, differences, precision=highest)
        return (
            shifts_here[:, None, None] * field
            - laplacian(field, factors, second)
            + penalty_weight * penalty
        )

    applied = operator(velocity)
    right_side = helm_shift * (velocity - time_step * advection)
    state = velocity
    for sweep in range(ITERS):
        state = state + relaxation * (right_side - applied) / precond[:, None, :]
        if sweep + 1 < ITERS:
            applied = operator(state)
    return (state, advection)


def solution(mesh):
    return jax.shard_map(
        body,
        mesh=mesh,
        in_specs=(
            P(None, "modes", None, "mesh"),
            P(None, "mesh"),
            P("mesh", None),
            P("mesh", None),
            P("mesh", None),
        ),
        out_specs=(P(None, "modes", None, "mesh"), P(None, "modes", None, "mesh")),
        check_vma=False,
    )
```

profile of v0, /device:TPU:1, one launch (start us, length us, event | category | flops | bytes accessed | tf_op | source)
XLA Modules:
  0.0 695.6 jit_solution(6972478493428846007)
XLA Ops:
  5.0 3.8 fusion.37
  15.9 4.1 pad_maximum_fusion
  19.9 36.6 %copy.166 = f32[12,16,81,128]{1,0,3,2:T(8,128)} copy(f32[12,16,81,128]{3,2,1,0:T(8,128)} %pad_maximum_fusion) | data formatting | bytes 15925248 | tf_op jit(solution)/shard_map/reshape | solution.py:160
  56.5 71.0 %reshape.346 = f32[8,1,248832]{2,1,0:T(1,128)} reshape(f32[10368,12,16]{2,1,0:T(8,128)} %bitcast.231) | data formatting | bytes 15925248
  127.5 5.4 all-to-all-start
  133.5 6.2 copy.127
  139.8 7.4 %slice_bitcast_fusion.7 = (f32[3,16,9,128]{1,0,3,2:T(4,128)}, f32[3,16,9,128]{1,0,3,2:T(4,128)}, f32[3,16,9,128]{1,0,3,2:T(4,128)}, f32[3,16,9,128]{1,0,3,2:T(4,128)}) fusion(f32[3,16,4,9,128]{1,0,4,3,2:T(4,128)} %bitcast.266), kind=kLoop, calls=%fused_computation.30 | loop fusion | bytes 1769472 | tf_op jit(solution)/shard_map/squeeze | solution.py:194
  147.2 4.1 gather_fusion.2
  153.9 4.9 collective-permute-start
  158.8 4.1 gather_fusion.6
  166.8 5.4 gather_fusion.4
  172.2 5.3 gather_fusion.8
  177.6 5.4 gather_fusion.9
  183.0 5.3 gather_fusion.5
  194.5 4.0 fusion.33
  211.5 7.4 %all-to-all-done = f32[8,1,248832]{2,1,0:T(1,128)} async-done(((f32[8,1,248832]{2,1,0:T(1,128)}), f32[8,1,248832]{2,1,0:T(1,128)}, u32[]{:S(2)}, u32[]{:S(2)}) %all-to-all-start) | async-done | bytes 7962656 | tf_op jit(solution)/shard_map/all_to_all | solution.py:163
  219.5 86.1 %reduce = f32[8,248832]{1,0:T(8,128)} reduce(f32[8,1,248832]{2,1,0:T(1,128)} %all-to-all-done, f32[]{:T(128)} %broadcast.263), dimensions={1}, to_apply=%all_to_all.6.reduce_sub_computation | reduce | bytes 15925252 | tf_op jit(solution)/shard_map/all_to_all | solution.py:163
  305.5 71.5 %reshape.347 = f32[10368,12,16]{2,1,0:T(8,128)} reshape(f32[8,248832]{1,0:T(8,128)} %reduce) | data formatting | bytes 15925248
  377.0 42.1 %copy.167 = f32[12,16,8,1296]{3,2,1,0:T(8,128)} copy(f32[12,16,8,1296]{1,0,3,2:T(8,128)} %bitcast.14) | data formatting | bytes 15925248 | tf_op jit(solution)/shard_map/reshape | solution.py:168
  419.1 16.5 %convolution_bitcast_fusion = f32[12,128,1296]{1,2,0:T(8,128)S(1)} fusion(f32[12,16,8,1296]{3,2,1,0:T(8,128)} %copy.167, f32[128,8,16,1]{0,1,2,3:T(8,128)S(1)} %copy-done.69), kind=kOutput, calls=%fused_computation.21 | convolution fusion | flops 3057647616 | bytes 15990784 | tf_op jit(solution)/shard_map/psc,fcsn->fpn/dot_general | solution.py:165
  436.4 4.0 convolution_bitcast_fusion.1
  440.5 18.0 %copy.168 = f32[3,16,8,1296]{1,0,3,2:T(4,128)} copy(f32[3,16,8,1296]{3,1,2,0:T(8,128)} %convolution_bitcast_fusion.1) | data formatting | bytes 3981312 | tf_op jit(solution)/shard_map/reshape | solution.py:172
  458.5 16.1 %reshape.348 = f32[8,1,62208]{2,1,0:T(1,128)} reshape(f32[10368,3,16]{2,1,0:T(4,128)} %bitcast.265) | data formatting | bytes 3981312
  474.6 8.2 %all-to-all-start.1 = ((f32[8,1,62208]{2,1,0:T(1,128)}), f32[8,1,62208]{2,1,0:T(1,128)}, u32[]{:S(2)}, u32[]{:S(2)}) async-start(f32[8,1,62208]{2,1,0:T(1,128)} %reshape.348), calls=%async_computation.1 | async-start | bytes 3981312 | tf_op jit(solution)/shard_map/all_to_all | solution.py:175
  482.8 4.2 fusion.11
  496.6 10.9 %maximum_subtract_fusion = f32[3,16,4,9,128]{1,0,4,3,2:T(4,128)} fusion(f32[3,16,4,9,128]{1,0,4,3,2:T(4,128)} %bitcast.267, f32[3,16,1,9,128]{1,0,4,3,2:T(4,128)S(1)} %copy-done.2, f32[3,16,1,9,128]{1,0,4,3,2:T(4,128)S(1)} %fusion.8, f32[3,16,1,9,128]{1,0,4,3,2:T(4,128)S(1)} %copy-done.3, f32[3,16,1,9,128]{1,0,4,3,2:T(4,128)S(1)} %copy-done.4), kind=kLoop, calls=%fused_computation.18 | loop fusion | flops 884736 | bytes 2654208 | tf_op jit(solution)/shard_map/sub | solution.py:210
  507.5 6.0 copy.139
  513.6 8.2 %reduce.1 = f32[8,62208]{1,0:T(8,128)} reduce(f32[8,1,62208]{2,1,0:T(1,128)} %all-to-all-done.1, f32[]{:T(128)} %broadcast.263), dimensions={1}, to_apply=%all_to_all.7.reduce_sub_computation | reduce | bytes 3981316 | tf_op jit(solution)/shard_map/all_to_all | solution.py:175
  521.8 25.0 %reshape.349 = f32[10368,3,16]{2,1,0:T(4,128)} reshape(f32[8,62208]{1,0:T(8,128)} %reduce.1) | data formatting | bytes 3981312
  546.8 13.1 %copy.169 = f32[3,16,81,128]{3,2,1,0:T(8,128)} copy(f32[3,16,81,128]{1,0,3,2:T(4,128)} %bitcast.263) | data formatting | bytes 3981312 | tf_op jit(solution)/shard_map/reshape | solution.py:175
  559.9 6.9 fusion.19
  577.5 6.8 copy.142
  584.4 7.4 %slice_bitcast_fusion.3 = (f32[3,16,9,128]{1,0,3,2:T(4,128)}, f32[3,16,9,128]{1,0,3,2:T(4,128)}, f32[3,16,9,128]{1,0,3,2:T(4,128)}, f32[3,16,9,128]{1,0,3,2:T(4,128)}) fusion(f32[3,16,4,9,128]{1,0,4,3,2:T(4,128)} %bitcast.268), kind=kLoop, calls=%fused_computation.26 | loop fusion | bytes 1769472 | tf_op jit(solution)/shard_map/squeeze | solution.py:194
  591.7 4.2 gather_fusion.10
  597.8 4.6 collective-permute-start.2
  602.4 4.2 gather_fusion.14
  610.7 5.0 fusion.45
  615.7 5.4 gather_fusion.12
  621.1 5.4 gather_fusion.16
  626.5 15.9 %copy.156 = f32[3,16,81,128]{3,1,2,0:T(8,128)} copy(f32[3,16,81,128]{1,0,3,2:T(4,128)} %bitcast.264) | data formatting | bytes 3981312
  642.4 5.4 gather_fusion.13
  647.9 5.4 gather_fusion.17
  654.7 3.9 gather_fusion.11
  663.8 5.4 fusion.3
  669.3 4.3 fusion
  673.6 6.4 maximum_subtract_fusion.1
  680.0 6.1 copy.154
  686.1 7.6 %fusion.15 = f32[3,16,81,128]{3,2,1,0:T(8,128)S(1)} fusion(f32[3,16,81,128]{3,2,1,0:T(8,128)} %copy-done.1, f32[3,16,128,81]{2,3,1,0:T(8,128)} %fusion.45, f32[3,16,128,81]{2,3,1,0:T(8,128)} %fusion.44, f32[3,16,128,81]{2,3,1,0:T(8,128)} %fusion.43, f32[3,16,81,128]{3,2,1,0:T(8,128)} %copy.169, f32[3,16,36,128]{3,2,1,0:T(8,128)S(1)} %copy.154, ...), kind=kOutput, calls=%fused_computation.67 | convolution fusion | flops 222953472 | bytes 14840784 | tf_op jit(solution)/shard_map/qt,fcte->fcqe/dot_general | solution.py:213
  (208 shorter events, 73.5 us)
Async XLA Ops:
  127.5 91.4 %all-to-all-start = ((f32[8,1,248832]{2,1,0:T(1,128)}), f32[8,1,248832]{2,1,0:T(1,128)}, u32[]{:S(2)}, u32[]{:S(2)}) async-start(f32[8,1,248832]{2,1,0:T(1,128)} %reshape.346), calls=%async_computation | async-start | bytes 15925248 | tf_op jit(solution)/shard_map/all_to_all | solution.py:163
  132.9 6.8 copy-start.17
  139.8 11.5 %copy-start.39 = (pred[64]{0:T(512)(128)(4,1)}, pred[64]{0:T(512)(128)(4,1)S(1)}, u32[]{:S(2)}) copy-start(pred[64]{0:T(512)(128)(4,1)S(1)} %get-tuple-element.17) | copy-start | bytes 196
  139.8 23.2 %copy-start.37 = (pred[64]{0:T(512)(128)(4,1)}, pred[64]{0:T(512)(128)(4,1)S(1)}, u32[]{:S(2)}) copy-start(pred[64]{0:T(512)(128)(4,1)S(1)} %get-tuple-element.64) | copy-start | bytes 196
  139.8 7.4 %copy-start.21 = (s32[1024]{0:T(1024)}, s32[1024]{0:T(1024)S(1)}, u32[]{:S(2)}) copy-start(s32[1024]{0:T(1024)S(1)} %pad_clamp_fusion.7) | copy-start | bytes 12292
  153.9 52.5 %collective-permute-start = (f32[3,16,9,64]{3,1,2,0:T(8,128)}, f32[3,16,9,64]{3,1,2,0:T(8,128)}, u32[]{:S(2)}, u32[]{:S(2)}) collective-permute-start(f32[3,16,9,64]{3,1,2,0:T(8,128)} %copy.128), channel_id=1, source_target_pairs={{0,8},{8,16},{16,24},{1,9},{9,17},{17,25},{2,10},{10,18},{18,26},{... | collective-permute-start | bytes 331784 | tf_op jit(solution)/shard_map/ppermute | solution.py:32
  158.8 7.9 %copy-start.20 = (s32[128,4]{0,1:T(4,128)S(1)}, s32[128,4]{0,1:T(4,128)}, u32[]{:S(2)}) copy-start(s32[128,4]{0,1:T(4,128)} %param.24) | copy-start | bytes 6148
  162.9 14.6 %copy-start.70 = (f32[128]{0:T(128)S(1)}, f32[128]{0:T(128)}, u32[]{:S(2)}) copy-start(f32[128]{0:T(128)} %constant.92.clone) | copy-start | bytes 1540
  164.5 23.8 %copy-start.57 = (s32[128,2]{0,1:T(2,128)S(1)}, s32[128,2]{0,1:T(2,128)}, u32[]{:S(2)}) copy-start(s32[128,2]{0,1:T(2,128)} %param.26) | copy-start | bytes 3076
  164.5 24.9 %copy-start.19 = (f32[4,128]{1,0:T(4,128)S(1)}, f32[4,128]{1,0:T(4,128)}, u32[]{:S(2)}) copy-start(f32[4,128]{1,0:T(4,128)} %param.23) | copy-start | bytes 6148
  164.6 26.1 %copy-start.11 = (f32[81,81,1,1]{1,0,3,2:T(8,128)S(1)}, f32[81,81,1,1]{1,0,3,2:T(8,128)}, u32[]{:S(2)}) copy-start(f32[81,81,1,1]{1,0,3,2:T(8,128)} %constant.112) | copy-start | bytes 78736
  164.9 322.1 %collective-permute-start.1 = (f32[3,16,9,64]{3,1,2,0:T(8,128)S(1)}, f32[3,16,9,64]{3,1,2,0:T(8,128)}, u32[]{:S(2)}, u32[]{:S(2)}) collective-permute-start(f32[3,16,9,64]{3,1,2,0:T(8,128)S(1)} %copy.133), channel_id=1, source_target_pairs={{8,0},{16,8},{24,16},{9,1},{17,9},{25,17},{10,2},{18,10},{26,18},{... | collective-permute-start | bytes 331784 | tf_op jit(solution)/shard_map/ppermute | solution.py:32
  166.8 35.5 %copy-start.29 = (pred[128]{0:T(512)(128)(4,1)}, pred[128]{0:T(512)(128)(4,1)S(1)}, u32[]{:S(2)}) copy-start(pred[128]{0:T(512)(128)(4,1)S(1)} %get-tuple-element.54) | copy-start | bytes 388
  166.8 37.6 %copy-start.35 = (pred[128]{0:T(512)(128)(4,1)}, pred[128]{0:T(512)(128)(4,1)S(1)}, u32[]{:S(2)}) copy-start(pred[128]{0:T(512)(128)(4,1)S(1)} %get-tuple-element.58) | copy-start | bytes 388
  166.8 315.9 %copy-start.33 = (pred[128]{0:T(512)(128)(4,1)}, pred[128]{0:T(512)(128)(4,1)S(1)}, u32[]{:S(2)}) copy-start(pred[128]{0:T(512)(128)(4,1)S(1)} %get-tuple-element.15) | copy-start | bytes 388
  166.8 325.3 %copy-start.31 = (pred[128]{0:T(512)(128)(4,1)}, pred[128]{0:T(512)(128)(4,1)S(1)}, u32[]{:S(2)}) copy-start(pred[128]{0:T(512)(128)(4,1)S(1)} %get-tuple-element.56) | copy-start | bytes 388
  166.8 10.7 %copy-start.24 = (s32[1024]{0:T(1024)}, s32[1024]{0:T(1024)S(1)}, u32[]{:S(2)}) copy-start(s32[1024]{0:T(1024)S(1)} %pad_clamp_fusion.5) | copy-start | bytes 12292
  172.2 18.5 %copy-start.25 = (s32[1024]{0:T(1024)}, s32[1024]{0:T(1024)S(1)}, u32[]{:S(2)}) copy-start(s32[1024]{0:T(1024)S(1)} %pad_clamp_fusion.1) | copy-start | bytes 12292
  177.6 13.1 %copy-start.58 = (f32[16]{0:T(128)}, f32[16]{0:T(128)S(1)}, u32[]{:S(2)}) copy-start(f32[16]{0:T(128)S(1)} %dynamic_slice.7) | copy-start | bytes 196
  177.6 11.9 %copy-start.23 = (s32[1024]{0:T(1024)}, s32[1024]{0:T(1024)S(1)}, u32[]{:S(2)}) copy-start(s32[1024]{0:T(1024)S(1)} %pad_clamp_fusion) | copy-start | bytes 12292
  183.0 7.7 %copy-start.27 = (s32[1024]{0:T(1024)}, s32[1024]{0:T(1024)S(1)}, u32[]{:S(2)}) copy-start(s32[1024]{0:T(1024)S(1)} %pad_clamp_fusion.4) | copy-start | bytes 12292
  188.9 303.2 %copy-start.41 = (pred[128]{0:T(512)(128)(4,1)}, pred[128]{0:T(512)(128)(4,1)S(1)}, u32[]{:S(2)}) copy-start(pred[128]{0:T(512)(128)(4,1)S(1)} %get-tuple-element.62) | copy-start | bytes 388
  188.9 18.9 %copy-start.26 = (s32[1024]{0:T(1024)}, s32[1024]{0:T(1024)S(1)}, u32[]{:S(2)}) copy-start(s32[1024]{0:T(1024)S(1)} %pad_clamp_fusion.6) | copy-start | bytes 12292
  190.6 11.7 %copy-start.49 = (f32[128]{0:T(128)}, f32[128]{0:T(128)S(1)}, u32[]{:S(2)}) copy-start(f32[128]{0:T(128)S(1)} %get-tuple-element.51) | copy-start | bytes 1540
  190.6 13.7 %copy-start.55 = (f32[128]{0:T(128)}, f32[128]{0:T(128)S(1)}, u32[]{:S(2)}) copy-start(f32[128]{0:T(128)S(1)} %get-tuple-element.53) | copy-start | bytes 1540
  206.4 282.0 %copy-start.28 = (s32[1024]{0:T(1024)}, s32[1024]{0:T(1024)S(1)}, u32[]{:S(2)}) copy-start(s32[1024]{0:T(1024)S(1)} %pad_clamp_fusion.2) | copy-start | bytes 12292
  377.0 42.1 %copy-start.69 = (f32[128,8,16,1]{0,1,2,3:T(8,128)S(1)}, f32[128,8,16,1]{0,1,2,3:T(8,128)}, u32[]{:S(2)}) copy-start(f32[128,8,16,1]{0,1,2,3:T(8,128)} %constant.109) | copy-start | bytes 196612
  474.6 8.2 %copy-start.45 = (pred[128]{0:T(512)(128)(4,1)S(1)}, pred[128]{0:T(512)(128)(4,1)}, u32[]{:S(2)}) copy-start(pred[128]{0:T(512)(128)(4,1)} %get-tuple-element.13) | copy-start | bytes 388
  474.6 8.2 %copy-start.47 = (pred[128]{0:T(512)(128)(4,1)S(1)}, pred[128]{0:T(512)(128)(4,1)}, u32[]{:S(2)}) copy-start(pred[128]{0:T(512)(128)(4,1)} %get-tuple-element.60) | copy-start | bytes 388
  474.6 8.2 %copy-start.53 = (f32[128]{0:T(128)S(1)}, f32[128]{0:T(128)}, u32[]{:S(2)}) copy-start(f32[128]{0:T(128)} %get-tuple-element.50) | copy-start | bytes 1540
  474.6 39.0 %all-to-all-start.1 = ((f32[8,1,62208]{2,1,0:T(1,128)}), f32[8,1,62208]{2,1,0:T(1,128)}, u32[]{:S(2)}, u32[]{:S(2)}) async-start(f32[8,1,62208]{2,1,0:T(1,128)} %reshape.348), calls=%async_computation.1 | async-start | bytes 3981312 | tf_op jit(solution)/shard_map/all_to_all | solution.py:175
  546.7 13.1 %copy-start.16 = (f32[81,36,1,1]{0,1,3,2:T(8,128)S(1)}, f32[81,36,1,1]{0,1,3,2:T(8,128)}, u32[]{:S(2)}) copy-start(f32[81,36,1,1]{0,1,3,2:T(8,128)} %constant.114) | copy-start | bytes 34996
  546.7 13.1 %copy-start.59 = (f32[16]{0:T(128)S(1)}, f32[16]{0:T(128)}, u32[]{:S(2)}) copy-start(f32[16]{0:T(128)} %copy-done.58) | copy-start | bytes 196
  546.7 13.1 %copy-start.61 = (f32[128]{0:T(128)S(1)}, f32[128]{0:T(128)}, u32[]{:S(2)}) copy-start(f32[128]{0:T(128)} %get-tuple-element.47) | copy-start | bytes 1540
  546.7 13.2 %copy-start.63 = (f32[128]{0:T(128)S(1)}, f32[128]{0:T(128)}, u32[]{:S(2)}) copy-start(f32[128]{0:T(128)} %get-tuple-element.48) | copy-start | bytes 1540
  546.7 13.2 %copy-start.65 = (f32[128]{0:T(128)S(1)}, f32[128]{0:T(128)}, u32[]{:S(2)}) copy-start(f32[128]{0:T(128)} %get-tuple-element.49) | copy-start | bytes 1540
  584.4 11.6 %copy-start.40 = (pred[64]{0:T(512)(128)(4,1)S(1)}, pred[64]{0:T(512)(128)(4,1)}, u32[]{:S(2)}) copy-start(pred[64]{0:T(512)(128)(4,1)} %copy-done.39) | copy-start | bytes 196
  595.9 10.7 %copy-start.38 = (pred[64]{0:T(512)(128)(4,1)S(1)}, pred[64]{0:T(512)(128)(4,1)}, u32[]{:S(2)}) copy-start(pred[64]{0:T(512)(128)(4,1)} %copy-done.37) | copy-start | bytes 196
  597.8 55.5 %collective-permute-start.2 = (f32[3,16,9,64]{3,1,2,0:T(8,128)S(1)}, f32[3,16,9,64]{3,1,2,0:T(8,128)}, u32[]{:S(2)}, u32[]{:S(2)}) collective-permute-start(f32[3,16,9,64]{3,1,2,0:T(8,128)S(1)} %copy.143), channel_id=1, source_target_pairs={{0,8},{8,16},{16,24},{1,9},{9,17},{17,25},{2,10},{10,18},{18,26},{... | collective-permute-start | bytes 331784 | tf_op jit(solution)/shard_map/ppermute | solution.py:32
  609.2 49.3 %collective-permute-start.3 = (f32[3,16,9,64]{3,1,2,0:T(8,128)}, f32[3,16,9,64]{3,1,2,0:T(8,128)}, u32[]{:S(2)}, u32[]{:S(2)}) collective-permute-start(f32[3,16,9,64]{3,1,2,0:T(8,128)} %copy.148), channel_id=1, source_target_pairs={{8,0},{16,8},{24,16},{9,1},{17,9},{25,17},{10,2},{18,10},{26,18},{... | collective-permute-start | bytes 331784 | tf_op jit(solution)/shard_map/ppermute | solution.py:32
  653.3 10.4 %copy-start.34 = (pred[128]{0:T(512)(128)(4,1)S(1)}, pred[128]{0:T(512)(128)(4,1)}, u32[]{:S(2)}) copy-start(pred[128]{0:T(512)(128)(4,1)} %copy-done.33) | copy-start | bytes 388
  653.3 10.4 %copy-start.36 = (pred[128]{0:T(512)(128)(4,1)S(1)}, pred[128]{0:T(512)(128)(4,1)}, u32[]{:S(2)}) copy-start(pred[128]{0:T(512)(128)(4,1)} %copy-done.35) | copy-start | bytes 388
  653.3 10.4 %copy-start.46 = (pred[128]{0:T(512)(128)(4,1)S(1)}, pred[128]{0:T(512)(128)(4,1)}, u32[]{:S(2)}) copy-start(pred[128]{0:T(512)(128)(4,1)} %get-tuple-element.13) | copy-start | bytes 388
  653.3 10.4 %copy-start.48 = (pred[128]{0:T(512)(128)(4,1)S(1)}, pred[128]{0:T(512)(128)(4,1)}, u32[]{:S(2)}) copy-start(pred[128]{0:T(512)(128)(4,1)} %get-tuple-element.60) | copy-start | bytes 388
  653.3 10.4 %copy-start.54 = (f32[128]{0:T(128)S(1)}, f32[128]{0:T(128)}, u32[]{:S(2)}) copy-start(f32[128]{0:T(128)} %get-tuple-element.50) | copy-start | bytes 1540
  653.3 10.4 %copy-start.56 = (f32[128]{0:T(128)S(1)}, f32[128]{0:T(128)}, u32[]{:S(2)}) copy-start(f32[128]{0:T(128)} %copy-done.55) | copy-start | bytes 1540
  663.8 9.8 %slice-start = ((s8[9437184]{0:T(1024)(128)(4,1)}), s8[4194304]{0:T(1024)(128)(4,1)S(1)}, s32[]{:S(2)}) async-start(s8[9437184]{0:T(1024)(128)(4,1)} %bitcast.269), calls=%async_computation.2 | async-start | bytes 8388608
  663.8 9.8 %slice-start.1 = ((s8[9437184]{0:T(1024)(128)(4,1)}), s8[4194304]{0:T(1024)(128)(4,1)S(1)}, s32[]{:S(2)}) async-start(s8[9437184]{0:T(1024)(128)(4,1)} %bitcast.269), calls=%async_computation.3 | async-start | bytes 8388608
  (32 other events, 142.7 us)
where the time goes:
time: 706 us; the launch traced here: 696 us
  local copies, waits for them, and re-layouts  447 us (63%)
  other arithmetic  146 us (21%)
  matrix products  67.4 us (10%)
  starting transfers between devices  26.3 us (4%)
  waiting for transfers between devices  7.46 us (1%)
    unnamed x155, local copies, waits for them, and re-layouts  208 us
    all_to_all x1, other arithmetic, body(): lax.all_to_all(stacked, 'modes', split_axis=2, concat_axis=2, tiled=True)  86.1 us
    gather x8, local copies, waits for them, and re-layouts, operator(): jnp.take(traces[:, :, opposite[edge_index]], picks[:, edge_index], axis=-1)  43 us
    reshape x1, local copies, waits for them, and re-layouts, body(): moved.reshape(12, local_coef, mode_count, point_count)  42.1 us
    reshape x1, local copies, waits for them, and re-layouts, body(): jnp.concatenate([velocity, grad_x, grad_y, grad_z], axis=0)  36.6 us
    another operation x6, other arithmetic, operator(): neighbours = jnp.stack(nearby, axis=2)  21.4 us
    reshape x1, local copies, waits for them, and re-layouts, body(): jnp.einsum('scp,fpn->fcsn', inverse_view, term, precision=highest)  18 us
    sub x2, other arithmetic, operator(): traces - neighbours  17.3 us
  transfers between devices with their start and end apart: 6, of which 1 were waited for; matrix products, arithmetic and copies ran while one was open for 59% of the time, Pallas kernels for 0%

commit v1 on v0

v1 whole, which is shorter than its diff:
```python
import functools

import jax
import jax.numpy as jnp
import ml_dtypes
import numpy as np
from jax import lax
from jax.experimental import pallas as pl
from jax.experimental.pallas import tpu as pltpu
from jax.sharding import PartitionSpec as P

COEF = 128
LANES = 128


highest = lax.Precision.HIGHEST
helm_shift = 4.0
penalty_weight = 200.0
spectral_bound = 400.0
relaxation = 0.8
time_step = 0.02
wave_scale = 0.125
gll_interior = [
    -0.8997579954114602,
    -0.6771862795107377,
    -0.3631174638261782,
    0.0,
    0.3631174638261782,
    0.6771862795107377,
    0.8997579954114602,
]


def shifted(block, axis, distance):
    devices = range(lax.axis_size(axis))
    route = [(i - distance, i) for i in devices if i - distance in devices]
    return lax.ppermute(block, axis, route)


def legendre_value(point, degree):
    previous = 1.0
    current = point
    for order_index in range(1, degree):
        following = ((2 * order_index + 1) * point * current - order_index * previous) / (
            order_index + 1
        )
        previous = current
        current = following
    return current


def spectral_tables(coef_count):
    poly_order = 8
    node_count = poly_order + 1
    points = np.array([-1.0] + gll_interior + [1.0])
    values = np.array([legendre_value(points[node], poly_order) for node in range(node_count)])
    derivative = np.zeros((node_count, node_count))
    for row_index in range(node_count):
        for col_index in range(node_count):
            if row_index != col_index:
                derivative[row_index, col_index] = values[row_index] / (
                    values[col_index] * (points[row_index] - points[col_index])
                )
    derivative[0, 0] = -poly_order * (poly_order + 1) / 4.0
    derivative[poly_order, poly_order] = poly_order * (poly_order + 1) / 4.0
    identity = np.eye(node_count)
    along_r = np.kron(identity, derivative)
    along_s = np.kron(derivative, identity)
    second = np.stack([along_r @ along_r, along_r @ along_s, along_s @ along_s])
    line_nodes = np.arange(node_count)
    edge_nodes = np.stack(
        [
            line_nodes,
            line_nodes * node_count + poly_order,
            poly_order * node_count + line_nodes,
            line_nodes * node_count,
        ]
    )
    counts = np.zeros(node_count * node_count)
    for edge_index in range(4):
        counts[edge_nodes[edge_index]] += 1.0
    planes = np.arange(coef_count) * 2.0 * np.pi / coef_count
    half_count = coef_count // 2
    wavenumber = np.zeros(coef_count)
    basis = np.zeros((coef_count, coef_count))
    z_derivative = np.zeros((coef_count, coef_count))
    basis[:, 0] = 1.0
    basis[:, 1] = np.cos(half_count * planes)
    wavenumber[1] = half_count
    for mode_number in range(1, half_count):
        basis[:, 2 * mode_number] = np.cos(mode_number * planes)
        basis[:, 2 * mode_number + 1] = np.sin(mode_number * planes)
        wavenumber[2 * mode_number] = mode_number
        wavenumber[2 * mode_number + 1] = mode_number
        z_derivative[2 * mode_number, 2 * mode_number + 1] = wave_scale * mode_number
        z_derivative[2 * mode_number + 1, 2 * mode_number] = -wave_scale * mode_number
    norms = np.full(coef_count, coef_count / 2.0)
    norms[0] = coef_count
    norms[1] = coef_count
    inverse = basis.T / norms[:, None]
    shifts = helm_shift + (wave_scale * wavenumber) ** 2
    return along_r, along_s, second, counts, basis, inverse, z_derivative, shifts


def split_table(table):
    exact = np.asarray(table, np.float64).astype(np.float32)
    high = exact.astype(ml_dtypes.bfloat16)
    low = (exact - high.astype(np.float32)).astype(ml_dtypes.bfloat16)
    return high, low


def pad_table(table, rows, cols):
    out = np.zeros((rows, cols))
    out[: table.shape[0], : table.shape[1]] = table
    return out


def split_value(value):
    high = value.astype(jnp.bfloat16)
    low = (value - high.astype(jnp.float32)).astype(jnp.bfloat16)
    return high, low


def mul(a, b):
    return jnp.dot(a, b, preferred_element_type=jnp.float32)


def row_ids():
    return lax.broadcasted_iota(jnp.int32, (8, LANES), 0)


def lane_ids():
    return lax.broadcasted_iota(jnp.int32, (8, LANES), 1)


def lane_take(value, index):
    return jnp.take_along_axis(value, index, axis=1, mode="promise_in_bounds")


def table_row(ref, row):
    return jnp.broadcast_to(ref[row : row + 1, :], (8, LANES))


def load_tile(ref, field, tile):
    if tile < 10:
        return ref[0, field, 8 * tile : 8 * tile + 8, :]
    last = jnp.broadcast_to(ref[0, field, 80:81, :], (8, LANES))
    return jnp.where(row_ids() == 0, last, 0.0)


def store_tile(ref, field, tile, value):
    if tile < 10:
        ref[0, field, 8 * tile : 8 * tile + 8, :] = value
    else:
        ref[0, field, 80:81, :] = value[0:1, :]


def swap_groups(planes):
    group = lane_ids() // 16
    planes = list(planes)
    for bit in (1, 2, 4):
        upper = (group & bit) != 0
        for i in range(8):
            if i & bit:
                continue
            j = i | bit
            first, second = planes[i], planes[j]
            planes[i] = jnp.where(upper, pltpu.roll(second, 16 * bit, 1), first)
            planes[j] = jnp.where(upper, second, pltpu.roll(first, LANES - 16 * bit, 1))
    return planes


def emit_halo(field_ref, table_ref, down_ref, up_ref, fields):
    pairs = fields // 2
    left = lane_ids() < 64
    for ref, table, base in ((down_ref, 6, 0), (up_ref, 7, 72)):
        index = table_row(table_ref, table)
        for pair in range(pairs):
            a, b = 2 * pair, 2 * pair + 1
            main = jnp.where(
                left,
                lane_take(field_ref[0, a, base : base + 8, :], index),
                lane_take(field_ref[0, b, base : base + 8, :], index),
            )
            ref[0, 8 * pair : 8 * pair + 8, :] = main
            rest_a = jnp.broadcast_to(field_ref[0, a, base + 8 : base + 9, :], (8, LANES))
            rest_b = jnp.broadcast_to(field_ref[0, b, base + 8 : base + 9, :], (8, LANES))
            rest = jnp.where(left, lane_take(rest_a, index), lane_take(rest_b, index))
            ref[0, 8 * pairs + pair : 8 * pairs + pair + 1, :] = rest[0:1, :]


def factor_rows(metrics_ref):
    rx, ry, sx, sy = (table_row(metrics_ref, k) for k in range(4))
    return rx * rx + ry * ry, 2.0 * (rx * sx + ry * sy), sx * sx + sy * sy


def pack_kernel(fields, packed, table_ref, x_ref, *outs):
    if packed:
        out_ref, down_ref, up_ref = outs
        for block in range(fields // 8):
            for tile in range(11):
                planes = swap_groups([load_tile(x_ref, 8 * block + g, tile) for g in range(8)])
                for g in range(8):
                    start = 88 * block + 8 * tile
                    out_ref[g, start : start + 8, :] = planes[g]
    else:
        down_ref, up_ref = outs
    emit_halo(x_ref, table_ref, down_ref, up_ref, fields)


def apply_operator(
    fields, shift_ref, metrics_ref, table_ref, ah_ref, al_ref, diag_ref, x_ref, low_ref, top_ref, finish
):
    pairs = fields // 2
    start = lax.axis_index("modes") * fields
    fa, fb, fc = factor_rows(metrics_ref)
    base = spectral_bound * (fa + fc) + penalty_weight
    raw = [table_row(table_ref, k) for k in range(6)]
    index = [jnp.maximum(r, 0) for r in raw]
    valid = [r >= 0 for r in raw]
    rows = row_ids()

    def pair_step(pair, carry):
        tiles = [[load_tile(x_ref, 2 * pair + h, t) for t in range(11)] for h in range(2)]
        zero = jnp.zeros((8, LANES), jnp.float32)
        both = jnp.concatenate(
            [jnp.concatenate(tiles[h] + [zero], axis=0) for h in range(2)], axis=1
        )
        high, low = split_value(both)
        ah, al = ah_ref[...], al_ref[...]
        second = mul(ah, high) + (mul(ah, low) + mul(al, high))
        low_main = low_ref[0, pl.ds(pl.multiple_of(8 * pair, 8), 8), :]
        top_main = top_ref[0, pl.ds(pl.multiple_of(8 * pair, 8), 8), :]
        low_rest = jnp.broadcast_to(low_ref[0, pl.ds(8 * pairs + pair, 1), :], (8, LANES))
        top_rest = jnp.broadcast_to(top_ref[0, pl.ds(8 * pairs + pair, 1), :], (8, LANES))
        for h in range(2):
            x = tiles[h]
            field = 2 * pair + h
            shift = shift_ref[start + field]
            scale = relaxation / (base + shift)
            low_index = index[4] + 64 * h
            top_index = index[5] + 64 * h

            def bottom(source, halo):
                own = jnp.where(valid[0], lane_take(source, index[0]), 0.0)
                return jnp.where(valid[4], lane_take(halo, low_index), own)

            def top(source, halo):
                own = jnp.where(valid[2], lane_take(source, index[2]), 0.0)
                return jnp.where(valid[5], lane_take(halo, top_index), own)

            for t in range(11):
                near = zero
                if t > 0 and t != 9:
                    right = jnp.where(valid[1], lane_take(x[t - 1], index[1]), 0.0)
                    near = near + jnp.where((rows + 8 * t) % 9 == 8, right, 0.0)
                if t < 8 or t == 9:
                    left = jnp.where(valid[3], lane_take(x[t + 1], index[3]), 0.0)
                    near = near + jnp.where((rows + 8 * t) % 9 == 0, left, 0.0)
                if t == 0:
                    near = near + bottom(x[9], low_main)
                if t == 1:
                    near = near + jnp.where(rows == 0, bottom(x[10], low_rest), 0.0)
                if t == 9:
                    near = near + top(x[0], top_main)
                if t == 10:
                    near = near + jnp.where(rows == 0, top(x[1], top_rest), 0.0)
                lanes = slice(LANES * h, LANES * h + LANES)
                lap = (
                    fa * second[8 * t : 8 * t + 8, lanes]
                    + fb * second[88 + 8 * t : 96 + 8 * t, lanes]
                    + fc * second[176 + 8 * t : 184 + 8 * t, lanes]
                )
                count = diag_ref[8 * t : 8 * t + 8, :]
                applied = shift * x[t] - lap + penalty_weight * (count * x[t] - near)
                finish(field, t, x[t], applied, scale)
        return carry

    lax.fori_loop(0, pairs, pair_step, 0)


def first_kernel(
    fields, shift_ref, metrics_ref, table_ref, ah_ref, al_ref, diag_ref, x_ref, low_ref, top_ref, out_ref
):
    def finish(field, tile, x, applied, scale):
        store_tile(out_ref, field, tile, x + scale * (helm_shift * x - applied))

    apply_operator(
        fields, shift_ref, metrics_ref, table_ref, ah_ref, al_ref, diag_ref, x_ref, low_ref, top_ref, finish
    )


def last_kernel(
    fields,
    shift_ref,
    metrics_ref,
    table_ref,
    ah_ref,
    al_ref,
    diag_ref,
    x_ref,
    low_ref,
    top_ref,
    vel_ref,
    adv_ref,
    out_ref,
):
    def finish(field, tile, x, applied, scale):
        right = helm_shift * (
            load_tile(vel_ref, field, tile) - time_step * load_tile(adv_ref, field, tile)
        )
        store_tile(out_ref, field, tile, x + scale * (right - applied))

    apply_operator(
        fields, shift_ref, metrics_ref, table_ref, ah_ref, al_ref, diag_ref, x_ref, low_ref, top_ref, finish
    )


def state_kernel(fields, packed, shift_ref, metrics_ref, table_ref, adv_in_ref, part_ref, *outs):
    start = lax.axis_index("modes") * fields
    fa, _, fc = factor_rows(metrics_ref)
    base = spectral_bound * (fa + fc) + penalty_weight
    amount = relaxation * helm_shift * time_step
    if packed:
        adv_ref, state_ref, down_ref, up_ref = outs
        for block in range(fields // 8):
            weight = [amount / (base + shift_ref[start + 8 * block + g]) for g in range(8)]
            for tile in range(11):
                first = 88 * block + 8 * tile
                planes = swap_groups([adv_in_ref[g, first : first + 8, :] for g in range(8)])
                for g in range(8):
                    field = 8 * block + g
                    store_tile(adv_ref, field, tile, planes[g])
                    part = load_tile(part_ref, field, tile)
                    store_tile(state_ref, field, tile, part - weight[g] * planes[g])
    else:
        state_ref, down_ref, up_ref = outs
        for field in range(fields):
            weight = amount / (base + shift_ref[start + field])
            for tile in range(11):
                part = load_tile(part_ref, field, tile)
                store_tile(
                    state_ref, field, tile, part - weight * load_tile(adv_in_ref, field, tile)
                )
    emit_halo(state_ref, table_ref, down_ref, up_ref, fields)


def plane_kernel(
    metrics_ref, bh_ref, bl_ref, dh_ref, dl_ref, ih_ref, il_ref, in_ref, out_ref, y0, y1, y2
):
    stages = (y0, y1, y2)
    offset = lax.axis_index("modes") * 16

    def spread(source, carry):
        for f in range(3):
            for block in range(2):
                first = 88 * (2 * f + block)
                part = in_ref[source, first : first + 88, :]
                full = jnp.concatenate([part, jnp.zeros((40, LANES), jnp.float32)], axis=0)
                where = pl.multiple_of(source * 256 + block * 128, 128)
                stages[f][pl.ds(where, 128), :] = full.T
        return carry

    lax.fori_loop(0, 8, spread, 0)

    def element(e, carry):
        value = jnp.concatenate(
            [stages[f][pl.ds(e, 128, stride=16), :] for f in range(3)], axis=1
        )
        high, low = split_value(value)
        planes = mul(bh_ref[...], jnp.concatenate([high, low], axis=0)) + mul(bl_ref[...], high)
        u, v, w = (planes[:128, 128 * f : 128 * f + 128] for f in range(3))
        high, low = split_value(jnp.concatenate([u, v, w], axis=0))
        grads = mul(jnp.concatenate([high, low], axis=1), dh_ref[...]) + mul(high, dl_ref[...])
        rx, ry, sx, sy = (metrics_ref[k, offset + e] for k in range(4))
        along_r = rx * u + ry * v
        along_s = sx * u + sy * v
        terms = []
        for f in range(3):
            rows = slice(128 * f, 128 * f + 128)
            terms.append(
                along_r * grads[rows, :128]
                + along_s * grads[rows, 128:]
                + w * planes[128:, 128 * f : 128 * f + 128]
            )
        high, low = split_value(jnp.concatenate(terms, axis=1))
        back = mul(ih_ref[...], jnp.concatenate([high, low], axis=0)) + mul(il_ref[...], high)
        for f in range(3):
            stages[f][pl.ds(e, 128, stride=16), :] = back[:, 128 * f : 128 * f + 128]
        return carry

    lax.fori_loop(0, 16, element, 0)

    def gather(target, carry):
        for f in range(3):
            for block in range(2):
                first = 88 * (2 * f + block)
                where = pl.multiple_of(target * 256 + block * 128, 128)
                full = stages[f][pl.ds(where, 128), :]
                out_ref[target, first : first + 88, :] = full.T[:88, :]
        return carry

    lax.fori_loop(0, 8, gather, 0)


def plain_advection(velocity, metrics, tables, mode_count):
    along_r, along_s, basis, inverse, plane_z = tables
    share = velocity.shape[3] // mode_count
    mode_index = lax.axis_index("modes")
    local = lax.dynamic_slice_in_dim(metrics, mode_index * share, share, axis=1)
    field = lax.all_to_all(velocity, "modes", split_axis=3, concat_axis=1, tiled=True)
    physical = jnp.einsum("pc,fcqe->fpqe", basis, field, precision=highest)
    grad_z = jnp.einsum("pc,fcqe->fpqe", plane_z, field, precision=highest)
    grad_r = jnp.einsum("qr,fpre->fpqe", along_r, physical, precision=highest)
    grad_s = jnp.einsum("qr,fpre->fpqe", along_s, physical, precision=highest)
    grad_x = local[0] * grad_r + local[2] * grad_s
    grad_y = local[1] * grad_r + local[3] * grad_s
    term = physical[0] * grad_x + physical[1] * grad_y + physical[2] * grad_z
    spectral = jnp.einsum("cp,fpqe->fcqe", inverse, term, precision=highest)
    return lax.all_to_all(spectral, "modes", split_axis=1, concat_axis=3, tiled=True)


def body(velocity, metrics, connect, send_list, recv_slot):
    along_r, along_s, second, counts, basis, inverse, z_derivative, shifts = spectral_tables(COEF)
    mode_count = lax.axis_size("modes")
    mesh_index = lax.axis_index("mesh")
    fields = velocity.shape[1]
    elements = velocity.shape[3]
    packed = mode_count == 8
    own = jnp.where(
        connect < 0, -1, jnp.clip(connect - mesh_index * elements, 0, elements - 1)
    )
    table = jnp.concatenate(
        [own.T, recv_slot.T, jnp.concatenate([send_list, send_list], axis=1)], axis=0
    )
    shifts = jnp.asarray(shifts, jnp.float32)
    halo_rows = 8 * (fields // 2) + (fields // 2 + 7) // 8 * 8
    ah, al = split_table(
        np.concatenate([pad_table(second[k], 88, 96) for k in range(3)], axis=0)
    )
    diag = np.zeros((88, LANES), np.float32)
    diag[:81] = counts[:, None]

    field_shape = jax.ShapeDtypeStruct(velocity.shape, jnp.float32)
    halo_shape = jax.ShapeDtypeStruct((3, halo_rows, LANES), jnp.float32)
    pack_shape = jax.ShapeDtypeStruct((8, 6 * 88, LANES), jnp.float32)
    field_spec = pl.BlockSpec((1, fields, 81, LANES), lambda f: (f, 0, 0, 0))
    halo_spec = pl.BlockSpec((1, halo_rows, LANES), lambda f: (f, 0, 0))
    pack_spec = pl.BlockSpec((8, 176, LANES), lambda f: (0, f, 0))
    smem = pl.BlockSpec(memory_space=pltpu.SMEM)

    def whole(shape):
        return pl.BlockSpec(shape, lambda f: (0,) * len(shape))

    params = pltpu.CompilerParams(vmem_limit_bytes=48 << 20)
    metric_spec, table_spec = whole((4, LANES)), whole((8, LANES))
    operator_specs = [
        smem,
        metric_spec,
        table_spec,
        whole((264, 96)),
        whole((264, 96)),
        whole((88, LANES)),
        field_spec,
        halo_spec,
        halo_spec,
    ]
    operator_tables = (shifts, metrics, table, jnp.asarray(ah), jnp.asarray(al), jnp.asarray(diag))

    sent = pl.pallas_call(
        functools.partial(pack_kernel, fields, packed),
        grid=(3,),
        in_specs=[table_spec, field_spec],
        out_specs=([pack_spec] if packed else []) + [halo_spec, halo_spec],
        out_shape=([pack_shape] if packed else []) + [halo_shape, halo_shape],
        compiler_params=params,
    )(table, velocity)
    down, up = sent[-2:]
    if packed:
        moved = lax.all_to_all(sent[0], "modes", split_axis=0, concat_axis=0, tiled=True)
    low = shifted(up, "mesh", 1)
    top = shifted(down, "mesh", -1)
    part = pl.pallas_call(
        functools.partial(first_kernel, fields),
        grid=(3,),
        in_specs=operator_specs,
        out_specs=field_spec,
        out_shape=field_shape,
        compiler_params=params,
        cost_estimate=pl.CostEstimate(
            flops=2 * 10**9, bytes_accessed=4 * 10**6, transcendentals=0
        ),
    )(*operator_tables, velocity, low, top)

    plane_z = basis @ z_derivative
    if packed:
        bh, bl = split_table(np.concatenate([basis, plane_z], axis=0))
        dh, dl = split_table(
            np.concatenate(
                [pad_table(along_r.T, 128, 128), pad_table(along_s.T, 128, 128)], axis=1
            )
        )
        ih, il = split_table(inverse)
        vmem = pl.BlockSpec(memory_space=pltpu.VMEM)
        terms = pl.pallas_call(
            plane_kernel,
            in_specs=[smem] + [vmem] * 7,
            out_specs=vmem,
            out_shape=pack_shape,
            scratch_shapes=[pltpu.VMEM((2048, LANES), jnp.float32)] * 3,
            compiler_params=params,
        )(
            metrics,
            jnp.asarray(np.concatenate([bh, bh], axis=1)),
            jnp.asarray(bl),
            jnp.asarray(np.concatenate([dh, dh], axis=0)),
            jnp.asarray(dl),
            jnp.asarray(np.concatenate([ih, ih], axis=1)),
            jnp.asarray(il),
            moved,
        )
        adv_in = lax.all_to_all(terms, "modes", split_axis=0, concat_axis=0, tiled=True)
        adv_spec = pack_spec
    else:
        tables = [
            jnp.asarray(t, jnp.float32) for t in (along_r, along_s, basis, inverse, plane_z)
        ]
        adv_in = plain_advection(velocity, metrics, tables, mode_count)
        adv_spec = field_spec

    found = pl.pallas_call(
        functools.partial(state_kernel, fields, packed),
        grid=(3,),
        in_specs=[smem, metric_spec, table_spec, adv_spec, field_spec],
        out_specs=([field_spec] if packed else []) + [field_spec, halo_spec, halo_spec],
        out_shape=([field_shape] if packed else []) + [field_shape, halo_shape, halo_shape],
        compiler_params=params,
    )(shifts, metrics, table, adv_in, part)
    advection = found[0] if packed else adv_in
    state, down, up = found[-3:]
    low = shifted(up, "mesh", 1)
    top = shifted(down, "mesh", -1)
    new_velocity = pl.pallas_call(
        functools.partial(last_kernel, fields),
        grid=(3,),
        in_specs=operator_specs + [field_spec, field_spec],
        out_specs=field_spec,
        out_shape=field_shape,
        compiler_params=params,
    )(*operator_tables, state, low, top, velocity, advection)
    return (new_velocity, advection)


def solution(mesh):
    return jax.shard_map(
        body,
        mesh=mesh,
        in_specs=(
            P(None, "modes", None, "mesh"),
            P(None, "mesh"),
            P("mesh", None),
            P("mesh", None),
            P("mesh", None),
        ),
        out_specs=(P(None, "modes", None, "mesh"), P(None, "modes", None, "mesh")),
        check_vma=False,
    )
```

time: 706 us -> 125 us (0.18)
  the two profiles are of different devices: /device:TPU:1 before, /device:TPU:0 now
where the time goes in v1:
time: 125 us
  Pallas kernels  51.5 us (41%)
  blocking collectives  32.4 us (26%)
  waiting for transfers between devices  17.4 us (14%)
  starting transfers between devices  14.1 us (11%)
  local copies, waits for them, and re-layouts  8.37 us (7%)
    all_to_all x1, blocking collectives, body(): lax.all_to_all(sent[0], 'modes', split_axis=0, concat_axis=0, tiled=True)  32.4 us
    pallas_call x1, Pallas kernels, body(): pl.pallas_call(plane_kernel, in_specs=[smem] + [vmem] * 7, out_specs=vmem...  16.9 us
    pallas_call x1, Pallas kernels, body(): pl.pallas_call(functools.partial(state_kernel, fields, packed), grid=(3,)...  10.2 us
    ppermute x4, starting transfers between devices, shifted(): return lax.ppermute(block, axis, route)  9.57 us
    ppermute x4, waiting for transfers between devices, shifted(): return lax.ppermute(block, axis, route)  9.35 us
    pallas_call x1, Pallas kernels, body(): pl.pallas_call(functools.partial(pack_kernel, fields, packed), grid=(3,),...  8.81 us
    unnamed x39, local copies, waits for them, and re-layouts  8.37 us
    pallas_call x1, Pallas kernels, body(): pl.pallas_call(functools.partial(last_kernel, fields), grid=(3,), in_spec...  8.16 us
  transfers between devices with their start and end apart: 5, of which 4 were waited for; matrix products, arithmetic and copies ran while one was open for 1% of the time, Pallas kernels for 6%

profile of v1, /device:TPU:0, one launch (start us, length us, event | category | flops | bytes accessed | tf_op | source)
XLA Modules:
  0.0 124.8 jit_solution(17061291055568511544)
XLA Ops:
  0.6 0.0 copy-start.15
  0.6 0.0 copy-start.17
  0.7 0.0 copy-start.16
  0.7 2.2 %copy.17.x_ref.vel_ref = f32[3,16,81,128]{3,2,1,0:T(8,128)S(1)} copy(f32[3,16,81,128]{3,1,2,0:T(8,128)} %param.15) | data formatting | bytes 3981312 | tf_op args[0]
  2.9 0.0 copy-start
  2.9 0.0 copy-done.15
  2.9 0.0 copy-done.17
  2.9 0.0 copy-done.16
  2.9 0.1 add_add_fusion.table_ref
  3.0 8.8 %shard_map.158 = (f32[8,528,128]{2,1,0:T(8,128)S(1)}, f32[3,72,128]{2,1,0:T(8,128)S(1)}, f32[3,72,128]{2,1,0:T(8,128)S(1)}) custom-call(s32[8,128]{1,0:T(8,128)S(1)} %add_add_fusion.table_ref, f32[3,16,81,128]{3,2,1,0:T(8,128)S(1)} %copy.17.x_ref.vel_ref), custom_call_target="tpu_custom_call" | custom-call | tf_op jit(solution)/shard_map/pallas_call | solution.py:470
  11.8 0.0 copy-start.4
  11.9 0.0 copy-start.5
  11.9 0.0 copy-start.8
  11.9 0.0 copy-start.9
  11.9 0.0 copy-start.10
  11.9 0.0 copy-start.12
  11.9 0.0 copy-start.13
  11.9 32.4 %all_to_all.10.in_ref = f32[8,528,128]{2,1,0:T(8,128)S(1)} all-to-all(f32[8,528,128]{2,1,0:T(8,128)S(1)} %get-tuple-element.9), channel_id=1, replica_groups=mesh['mesh'=4,'modes'=8] {'modes'}, dimensions={0} | all-to-all | bytes 4325376 | tf_op jit(solution)/shard_map/all_to_all | solution.py:480
  44.3 0.0 copy-done.4
  44.3 0.0 copy-done.5
  44.3 0.0 copy-done.8
  44.3 0.0 copy-done.9
  44.3 0.0 copy-done.10
  44.4 0.0 copy-done.12
  44.4 0.0 copy-done.13
  44.4 16.9 %shard_map.159 = f32[8,528,128]{2,1,0:T(8,128)S(1)} custom-call(f32[4,128]{1,0:T(4,128)S(1)} %copy-done.13, bf16[256,256]{1,0:T(8,128)(2,1)S(1)} %copy-done.5, bf16[256,128]{1,0:T(8,128)(2,1)S(1)} %copy-done.10, bf16[256,256]{1,0:T(8,128)(2,1)S(1)} %copy-done.4, bf16[128,256]{1,0:T(8,128)(2,1)S(1)} %copy-done.9, bf16[128,256]{1,0:T(8,128)(2,1)S(1)} %copy-done.8, ...), custom_call_target="tpu_custom_call" | custom-call | tf_op jit(solution)/shard_map/pallas_call | solution.py:505
  61.3 0.0 copy-start.1
  61.3 1.4 %copy-done.1 = f32[8,528,128]{2,1,0:T(8,128)} copy-done((f32[8,528,128]{2,1,0:T(8,128)}, f32[8,528,128]{2,1,0:T(8,128)S(1)}, u32[]{:S(2)}) %copy-start.1) | copy-done | bytes 2162712
  62.7 4.5 %all-to-all-start.1 = ((f32[8,528,128]{2,1,0:T(8,128)}), f32[8,528,128]{2,1,0:T(8,128)}, u32[]{:S(2)}, u32[]{:S(2)}) async-start(f32[8,528,128]{2,1,0:T(8,128)} %copy-done.1), calls=%async_computation.1 | async-start | bytes 4325376 | tf_op jit(solution)/shard_map/all_to_all | solution.py:522
  67.2 3.5 %collective-permute-start = (f32[3,72,128]{2,1,0:T(8,128)S(1)}, f32[3,72,128]{2,1,0:T(8,128)S(1)}, u32[]{:S(2)}, u32[]{:S(2)}) collective-permute-start(f32[3,72,128]{2,1,0:T(8,128)S(1)} %get-tuple-element.10), channel_id=1, source_target_pairs={{0,8},{8,16},{16,24},{1,9},{9,17},{17,25},{2,10},{10,18},{18,26},{... | collective-permute-start | bytes 331784 | tf_op jit(solution)/shard_map/ppermute | solution.py:37
  70.8 1.3 %collective-permute-start.1 = (f32[3,72,128]{2,1,0:T(8,128)S(1)}, f32[3,72,128]{2,1,0:T(8,128)S(1)}, u32[]{:S(2)}, u32[]{:S(2)}) collective-permute-start(f32[3,72,128]{2,1,0:T(8,128)S(1)} %get-tuple-element.11), channel_id=1, source_target_pairs={{8,0},{16,8},{24,16},{9,1},{17,9},{25,17},{10,2},{18,10},{26,18},{... | collective-permute-start | bytes 331784 | tf_op jit(solution)/shard_map/ppermute | solution.py:37
  72.1 1.5 %collective-permute-done.low_ref = f32[3,72,128]{2,1,0:T(8,128)S(1)} collective-permute-done((f32[3,72,128]{2,1,0:T(8,128)S(1)}, f32[3,72,128]{2,1,0:T(8,128)S(1)}, u32[]{:S(2)}, u32[]{:S(2)}) %collective-permute-start) | collective-permute-done | bytes 110624 | tf_op jit(solution)/shard_map/ppermute | solution.py:37
  73.6 4.1 %collective-permute-done.1.top_ref = f32[3,72,128]{2,1,0:T(8,128)S(1)} collective-permute-done((f32[3,72,128]{2,1,0:T(8,128)S(1)}, f32[3,72,128]{2,1,0:T(8,128)S(1)}, u32[]{:S(2)}, u32[]{:S(2)}) %collective-permute-start.1) | collective-permute-done | bytes 110624 | tf_op jit(solution)/shard_map/ppermute | solution.py:37
  77.7 0.0 copy-done
  77.7 0.0 copy-done.6
  77.7 0.0 copy-done.7
  77.7 0.0 copy-done.11
  77.7 7.4 %shard_map.160.part_ref = f32[3,16,81,128]{3,2,1,0:T(8,128)S(1)} custom-call(f32[128]{0:T(128)S(1)} %copy-done.14, f32[4,128]{1,0:T(4,128)S(1)} %copy-done.13, s32[8,128]{1,0:T(8,128)S(1)} %add_add_fusion.table_ref, bf16[264,96]{1,0:T(8,128)(2,1)S(1)} %copy-done.7, bf16[264,96]{1,0:T(8,128)(2,1)S(1)} %copy-done.6, f32[88,128]{1,0:T(8,128)S(1)} %copy-done.11, ...), custom_call_target="tpu_custom_call" | custom-call | flops 2000000000 | bytes 4000000 | tf_op jit(solution)/shard_map/pallas_call | solution.py:483
  85.1 1.4 %copy-done.3 = f32[3,16,81,128]{3,2,1,0:T(8,128)} copy-done((f32[3,16,81,128]{3,2,1,0:T(8,128)}, f32[3,16,81,128]{3,2,1,0:T(8,128)S(1)}, u32[]{:S(2)}) %copy-start.3) | copy-done | bytes 1990680
  86.5 8.1 %all-to-all-done.1.adv_in_ref = f32[8,528,128]{2,1,0:T(8,128)} async-done(((f32[8,528,128]{2,1,0:T(8,128)}), f32[8,528,128]{2,1,0:T(8,128)}, u32[]{:S(2)}, u32[]{:S(2)}) %all-to-all-start.1) | async-done | bytes 2162720 | tf_op jit(solution)/shard_map/all_to_all | solution.py:522
  94.6 10.2 %shard_map.161 = (f32[3,16,81,128]{3,2,1,0:T(8,128)S(1)}, f32[3,16,81,128]{3,2,1,0:T(8,128)S(1)}, f32[3,72,128]{2,1,0:T(8,128)S(1)}, f32[3,72,128]{2,1,0:T(8,128)S(1)}) custom-call(f32[128]{0:T(128)S(1)} %copy-done.14, f32[4,128]{1,0:T(4,128)S(1)} %copy-done.13, s32[8,128]{1,0:T(8,128)S(1)} %add_add_fusion.table_ref, ...), custom_call_target="tpu_custom_call" | custom-call | tf_op jit(solution)/shard_map/pallas_call | solution.py:531
  104.8 3.5 %collective-permute-start.2 = (f32[3,72,128]{2,1,0:T(8,128)S(1)}, f32[3,72,128]{2,1,0:T(8,128)S(1)}, u32[]{:S(2)}, u32[]{:S(2)}) collective-permute-start(f32[3,72,128]{2,1,0:T(8,128)S(1)} %get-tuple-element.13), channel_id=1, source_target_pairs={{0,8},{8,16},{16,24},{1,9},{9,17},{17,25},{2,10},{10,18},{18,26},{... | collective-permute-start | bytes 331784 | tf_op jit(solution)/shard_map/ppermute | solution.py:37
  108.3 1.3 %collective-permute-start.3 = (f32[3,72,128]{2,1,0:T(8,128)S(1)}, f32[3,72,128]{2,1,0:T(8,128)S(1)}, u32[]{:S(2)}, u32[]{:S(2)}) collective-permute-start(f32[3,72,128]{2,1,0:T(8,128)S(1)} %get-tuple-element.14), channel_id=1, source_target_pairs={{8,0},{16,8},{24,16},{9,1},{17,9},{25,17},{10,2},{18,10},{26,18},{... | collective-permute-start | bytes 331784 | tf_op jit(solution)/shard_map/ppermute | solution.py:37
  109.6 1.6 %copy.21 = f32[3,16,81,128]{3,1,2,0:T(8,128)} copy(f32[3,16,81,128]{3,2,1,0:T(8,128)S(1)} %get-tuple-element.17.adv_ref) | data formatting | bytes 3981312
  111.3 0.0 collective-permute-done.2.low_ref
  111.3 3.7 %collective-permute-done.3.top_ref = f32[3,72,128]{2,1,0:T(8,128)S(1)} collective-permute-done((f32[3,72,128]{2,1,0:T(8,128)S(1)}, f32[3,72,128]{2,1,0:T(8,128)S(1)}, u32[]{:S(2)}, u32[]{:S(2)}) %collective-permute-start.3) | collective-permute-done | bytes 110624 | tf_op jit(solution)/shard_map/ppermute | solution.py:37
  115.0 8.2 %shard_map.162 = f32[3,16,81,128]{3,2,1,0:T(8,128)S(1)} custom-call(f32[128]{0:T(128)S(1)} %copy-done.14, f32[4,128]{1,0:T(4,128)S(1)} %copy-done.13, s32[8,128]{1,0:T(8,128)S(1)} %add_add_fusion.table_ref, bf16[264,96]{1,0:T(8,128)(2,1)S(1)} %copy-done.7, bf16[264,96]{1,0:T(8,128)(2,1)S(1)} %copy-done.6, f32[88,128]{1,0:T(8,128)S(1)} %copy-done.11, ...), custom_call_target="tpu_custom_call" | custom-call | tf_op jit(solution)/shard_map/pallas_call | solution.py:543
  123.1 1.6 %copy.20 = f32[3,16,81,128]{3,1,2,0:T(8,128)} copy(f32[3,16,81,128]{3,2,1,0:T(8,128)S(1)} %shard_map.162) | data formatting | bytes 3981312
  (9 shorter events, 0.0 us)
Async XLA Ops:
  0.6 2.3 %copy-start.15 = (s32[128,4]{0,1:T(4,128)S(1)}, s32[128,4]{0,1:T(4,128)}, u32[]{:S(2)}) copy-start(s32[128,4]{0,1:T(4,128)} %param.17) | copy-start | bytes 6148
  0.6 2.3 %copy-start.17 = (s32[128,2]{0,1:T(2,128)S(1)}, s32[128,2]{0,1:T(2,128)}, u32[]{:S(2)}) copy-start(s32[128,2]{0,1:T(2,128)} %param.19) | copy-start | bytes 3076
  0.7 2.3 %copy-start.16 = (s32[2,64]{1,0:T(2,128)S(1)}, s32[2,64]{1,0:T(2,128)}, u32[]{:S(2)}) copy-start(s32[2,64]{1,0:T(2,128)} %param.18) | copy-start | bytes 1540
  2.9 74.8 %copy-start = (f32[3,16,81,128]{3,2,1,0:T(8,128)}, f32[3,16,81,128]{3,2,1,0:T(8,128)S(1)}, u32[]{:S(2)}) copy-start(f32[3,16,81,128]{3,2,1,0:T(8,128)S(1)} %copy.17.x_ref.vel_ref) | copy-start | bytes 5971972
  11.8 32.5 %copy-start.4 = (bf16[256,256]{1,0:T(8,128)(2,1)S(1)}, bf16[256,256]{1,0:T(8,128)(2,1)}, u32[]{:S(2)}) copy-start(bf16[256,256]{1,0:T(8,128)(2,1)} %constant.40.clone.dh_ref) | copy-start | bytes 393220
  11.9 32.5 %copy-start.5 = (bf16[256,256]{1,0:T(8,128)(2,1)S(1)}, bf16[256,256]{1,0:T(8,128)(2,1)}, u32[]{:S(2)}) copy-start(bf16[256,256]{1,0:T(8,128)(2,1)} %constant.38.clone.bh_ref) | copy-start | bytes 393220
  11.9 32.5 %copy-start.8 = (bf16[128,256]{1,0:T(8,128)(2,1)S(1)}, bf16[128,256]{1,0:T(8,128)(2,1)}, u32[]{:S(2)}) copy-start(bf16[128,256]{1,0:T(8,128)(2,1)} %constant.42.clone.ih_ref) | copy-start | bytes 196612
  11.9 32.5 %copy-start.9 = (bf16[128,256]{1,0:T(8,128)(2,1)S(1)}, bf16[128,256]{1,0:T(8,128)(2,1)}, u32[]{:S(2)}) copy-start(bf16[128,256]{1,0:T(8,128)(2,1)} %constant.41.clone.dl_ref) | copy-start | bytes 196612
  11.9 32.5 %copy-start.10 = (bf16[256,128]{1,0:T(8,128)(2,1)S(1)}, bf16[256,128]{1,0:T(8,128)(2,1)}, u32[]{:S(2)}) copy-start(bf16[256,128]{1,0:T(8,128)(2,1)} %constant.39.clone.bl_ref) | copy-start | bytes 196612
  11.9 32.5 %copy-start.12 = (bf16[128,128]{1,0:T(8,128)(2,1)S(1)}, bf16[128,128]{1,0:T(8,128)(2,1)}, u32[]{:S(2)}) copy-start(bf16[128,128]{1,0:T(8,128)(2,1)} %constant.43.clone.il_ref) | copy-start | bytes 98308
  11.9 32.5 %copy-start.13 = (f32[4,128]{1,0:T(4,128)S(1)}, f32[4,128]{1,0:T(4,128)}, u32[]{:S(2)}) copy-start(f32[4,128]{1,0:T(4,128)} %metrics_ref.7) | copy-start | bytes 6148
  61.3 1.4 %copy-start.1 = (f32[8,528,128]{2,1,0:T(8,128)}, f32[8,528,128]{2,1,0:T(8,128)S(1)}, u32[]{:S(2)}) copy-start(f32[8,528,128]{2,1,0:T(8,128)S(1)} %shard_map.159) | copy-start | bytes 6488068
  62.7 15.0 %copy-start.6 = (bf16[264,96]{1,0:T(8,128)(2,1)S(1)}, bf16[264,96]{1,0:T(8,128)(2,1)}, u32[]{:S(2)}) copy-start(bf16[264,96]{1,0:T(8,128)(2,1)} %constant.36.clone.al_ref) | copy-start | bytes 152068
  62.7 15.0 %copy-start.7 = (bf16[264,96]{1,0:T(8,128)(2,1)S(1)}, bf16[264,96]{1,0:T(8,128)(2,1)}, u32[]{:S(2)}) copy-start(bf16[264,96]{1,0:T(8,128)(2,1)} %constant.35.clone.ah_ref) | copy-start | bytes 152068
  62.7 15.0 %copy-start.11 = (f32[88,128]{1,0:T(8,128)S(1)}, f32[88,128]{1,0:T(8,128)}, u32[]{:S(2)}) copy-start(f32[88,128]{1,0:T(8,128)} %constant.37.clone.diag_ref) | copy-start | bytes 135172
  62.7 15.0 %copy-start.14 = (f32[128]{0:T(128)S(1)}, f32[128]{0:T(128)}, u32[]{:S(2)}) copy-start(f32[128]{0:T(128)} %constant.34.clone.shift_ref) | copy-start | bytes 1540
  62.7 31.9 %all-to-all-start.1 = ((f32[8,528,128]{2,1,0:T(8,128)}), f32[8,528,128]{2,1,0:T(8,128)}, u32[]{:S(2)}, u32[]{:S(2)}) async-start(f32[8,528,128]{2,1,0:T(8,128)} %copy-done.1), calls=%async_computation.1 | async-start | bytes 4325376 | tf_op jit(solution)/shard_map/all_to_all | solution.py:522
  67.2 6.3 %collective-permute-start = (f32[3,72,128]{2,1,0:T(8,128)S(1)}, f32[3,72,128]{2,1,0:T(8,128)S(1)}, u32[]{:S(2)}, u32[]{:S(2)}) collective-permute-start(f32[3,72,128]{2,1,0:T(8,128)S(1)} %get-tuple-element.10), channel_id=1, source_target_pairs={{0,8},{8,16},{16,24},{1,9},{9,17},{17,25},{2,10},{10,18},{18,26},{... | collective-permute-start | bytes 331784 | tf_op jit(solution)/shard_map/ppermute | solution.py:37
  70.8 6.9 %collective-permute-start.1 = (f32[3,72,128]{2,1,0:T(8,128)S(1)}, f32[3,72,128]{2,1,0:T(8,128)S(1)}, u32[]{:S(2)}, u32[]{:S(2)}) collective-permute-start(f32[3,72,128]{2,1,0:T(8,128)S(1)} %get-tuple-element.11), channel_id=1, source_target_pairs={{8,0},{16,8},{24,16},{9,1},{17,9},{25,17},{10,2},{18,10},{26,18},{... | collective-permute-start | bytes 331784 | tf_op jit(solution)/shard_map/ppermute | solution.py:37
  85.1 1.4 %copy-start.3 = (f32[3,16,81,128]{3,2,1,0:T(8,128)}, f32[3,16,81,128]{3,2,1,0:T(8,128)S(1)}, u32[]{:S(2)}) copy-start(f32[3,16,81,128]{3,2,1,0:T(8,128)S(1)} %shard_map.160.part_ref) | copy-start | bytes 5971972
  104.8 10.2 %copy-start.2 = (f32[3,16,81,128]{3,2,1,0:T(8,128)}, f32[3,16,81,128]{3,2,1,0:T(8,128)S(1)}, u32[]{:S(2)}) copy-start(f32[3,16,81,128]{3,2,1,0:T(8,128)S(1)} %get-tuple-element.17.adv_ref) | copy-start | bytes 5971972
  104.8 6.4 %collective-permute-start.2 = (f32[3,72,128]{2,1,0:T(8,128)S(1)}, f32[3,72,128]{2,1,0:T(8,128)S(1)}, u32[]{:S(2)}, u32[]{:S(2)}) collective-permute-start(f32[3,72,128]{2,1,0:T(8,128)S(1)} %get-tuple-element.13), channel_id=1, source_target_pairs={{0,8},{8,16},{16,24},{1,9},{9,17},{17,25},{2,10},{10,18},{18,26},{... | collective-permute-start | bytes 331784 | tf_op jit(solution)/shard_map/ppermute | solution.py:37
  108.3 6.6 %collective-permute-start.3 = (f32[3,72,128]{2,1,0:T(8,128)S(1)}, f32[3,72,128]{2,1,0:T(8,128)S(1)}, u32[]{:S(2)}, u32[]{:S(2)}) collective-permute-start(f32[3,72,128]{2,1,0:T(8,128)S(1)} %get-tuple-element.14), channel_id=1, source_target_pairs={{8,0},{16,8},{24,16},{9,1},{17,9},{25,17},{10,2},{18,10},{26,18},{... | collective-permute-start | bytes 331784 | tf_op jit(solution)/shard_map/ppermute | solution.py:37

commit v2 on v1

v2 whole, which is shorter than its diff:
```python
import functools

import jax
import jax.numpy as jnp
import ml_dtypes
import numpy as np
from jax import lax
from jax.experimental import pallas as pl
from jax.experimental.pallas import tpu as pltpu
from jax.sharding import PartitionSpec as P

COEF = 128
LANES = 128
MESH = pl.DeviceIdType.MESH


highest = lax.Precision.HIGHEST
helm_shift = 4.0
penalty_weight = 200.0
spectral_bound = 400.0
relaxation = 0.8
time_step = 0.02
wave_scale = 0.125
gll_interior = [
    -0.8997579954114602,
    -0.6771862795107377,
    -0.3631174638261782,
    0.0,
    0.3631174638261782,
    0.6771862795107377,
    0.8997579954114602,
]


def shifted(block, axis, distance):
    devices = range(lax.axis_size(axis))
    route = [(i - distance, i) for i in devices if i - distance in devices]
    return lax.ppermute(block, axis, route)


def legendre_value(point, degree):
    previous = 1.0
    current = point
    for order_index in range(1, degree):
        following = ((2 * order_index + 1) * point * current - order_index * previous) / (
            order_index + 1
        )
        previous = current
        current = following
    return current


def spectral_tables(coef_count):
    poly_order = 8
    node_count = poly_order + 1
    points = np.array([-1.0] + gll_interior + [1.0])
    values = np.array([legendre_value(points[node], poly_order) for node in range(node_count)])
    derivative = np.zeros((node_count, node_count))
    for row_index in range(node_count):
        for col_index in range(node_count):
            if row_index != col_index:
                derivative[row_index, col_index] = values[row_index] / (
                    values[col_index] * (points[row_index] - points[col_index])
                )
    derivative[0, 0] = -poly_order * (poly_order + 1) / 4.0
    derivative[poly_order, poly_order] = poly_order * (poly_order + 1) / 4.0
    identity = np.eye(node_count)
    along_r = np.kron(identity, derivative)
    along_s = np.kron(derivative, identity)
    second = np.stack([along_r @ along_r, along_r @ along_s, along_s @ along_s])
    line_nodes = np.arange(node_count)
    edge_nodes = np.stack(
        [
            line_nodes,
            line_nodes * node_count + poly_order,
            poly_order * node_count + line_nodes,
            line_nodes * node_count,
        ]
    )
    counts = np.zeros(node_count * node_count)
    for edge_index in range(4):
        counts[edge_nodes[edge_index]] += 1.0
    planes = np.arange(coef_count) * 2.0 * np.pi / coef_count
    half_count = coef_count // 2
    wavenumber = np.zeros(coef_count)
    basis = np.zeros((coef_count, coef_count))
    z_derivative = np.zeros((coef_count, coef_count))
    basis[:, 0] = 1.0
    basis[:, 1] = np.cos(half_count * planes)
    wavenumber[1] = half_count
    for mode_number in range(1, half_count):
        basis[:, 2 * mode_number] = np.cos(mode_number * planes)
        basis[:, 2 * mode_number + 1] = np.sin(mode_number * planes)
        wavenumber[2 * mode_number] = mode_number
        wavenumber[2 * mode_number + 1] = mode_number
        z_derivative[2 * mode_number, 2 * mode_number + 1] = wave_scale * mode_number
        z_derivative[2 * mode_number + 1, 2 * mode_number] = -wave_scale * mode_number
    norms = np.full(coef_count, coef_count / 2.0)
    norms[0] = coef_count
    norms[1] = coef_count
    inverse = basis.T / norms[:, None]
    shifts = helm_shift + (wave_scale * wavenumber) ** 2
    return along_r, along_s, second, counts, basis, inverse, z_derivative, shifts


def split_table(table):
    exact = np.asarray(table, np.float64).astype(np.float32)
    high = exact.astype(ml_dtypes.bfloat16)
    low = (exact - high.astype(np.float32)).astype(ml_dtypes.bfloat16)
    return high, low


def pad_table(table, rows, cols):
    out = np.zeros((rows, cols))
    out[: table.shape[0], : table.shape[1]] = table
    return out


def split_value(value):
    high = value.astype(jnp.bfloat16)
    low = (value - high.astype(jnp.float32)).astype(jnp.bfloat16)
    return high, low


def mul(a, b):
    return jnp.dot(a, b, preferred_element_type=jnp.float32)


def row_ids():
    return lax.broadcasted_iota(jnp.int32, (8, LANES), 0)


def lane_ids():
    return lax.broadcasted_iota(jnp.int32, (8, LANES), 1)


def lane_take(value, index):
    return jnp.take_along_axis(value, index, axis=1, mode="promise_in_bounds")


def table_row(ref, row):
    return jnp.broadcast_to(ref[row : row + 1, :], (8, LANES))


class Field:
    def __init__(self, ref, part, stride=None):
        self.ref, self.part, self.stride = ref, part, stride

    def rows(self, field, first, count):
        if self.stride is None:
            return self.ref[self.part, field, first : first + count, :]
        start = first * self.stride + field
        if count == 1:
            return self.ref[self.part, pl.ds(start, 1), :]
        return self.ref[self.part, pl.ds(start, count, stride=self.stride), :]

    def spread_row(self, field, row):
        return jnp.broadcast_to(self.rows(field, row, 1), (8, LANES))

    def tile(self, field, tile):
        if tile < 10:
            return self.rows(field, 8 * tile, 8)
        return jnp.where(row_ids() == 0, self.spread_row(field, 80), 0.0)

    def put(self, field, tile, value):
        count = 8 if tile < 10 else 1
        value = value if tile < 10 else value[0:1, :]
        if self.stride is None:
            self.ref[self.part, field, 8 * tile : 8 * tile + count, :] = value
            return
        start = 8 * tile * self.stride + field
        if count == 1:
            self.ref[self.part, pl.ds(start, 1), :] = value
        else:
            self.ref[self.part, pl.ds(start, count, stride=self.stride), :] = value


def swap_groups(planes):
    group = lane_ids() // 8
    planes = list(planes)
    for bit in (1, 2, 4, 8):
        upper = (group & bit) != 0
        for i in range(16):
            if i & bit:
                continue
            j = i | bit
            first, second = planes[i], planes[j]
            planes[i] = jnp.where(upper, pltpu.roll(second, 8 * bit, 1), first)
            planes[j] = jnp.where(upper, second, pltpu.roll(first, LANES - 8 * bit, 1))
    return planes


def emit_halo(source, table_ref, down_ref, up_ref, part, fields):
    pairs = fields // 2
    left = lane_ids() < 64
    for ref, table, base in ((down_ref, 6, 0), (up_ref, 7, 72)):
        index = table_row(table_ref, table)
        for pair in range(pairs):
            a, b = 2 * pair, 2 * pair + 1
            main = jnp.where(
                left,
                lane_take(source.rows(a, base, 8), index),
                lane_take(source.rows(b, base, 8), index),
            )
            ref[part, 8 * pair : 8 * pair + 8, :] = main
            rest = jnp.where(
                left,
                lane_take(source.spread_row(a, base + 8), index),
                lane_take(source.spread_row(b, base + 8), index),
            )
            ref[part, 8 * pairs + pair : 8 * pairs + pair + 1, :] = rest[0:1, :]


def factor_rows(metrics_ref):
    rx, ry, sx, sy = (table_row(metrics_ref, k) for k in range(4))
    return rx * rx + ry * ry, 2.0 * (rx * sx + ry * sy), sx * sx + sy * sy


def halo_kernel(fields, table_ref, x_ref, down_ref, up_ref):
    emit_halo(Field(x_ref, 0, fields), table_ref, down_ref, up_ref, 0, fields)


def apply_operator(fields, operator, source, part, low_ref, top_ref, finish):
    shift_ref, metrics_ref, table_ref, ah_ref, al_ref, diag_ref = operator
    pairs = fields // 2
    start = lax.axis_index("modes") * fields
    fa, fb, fc = factor_rows(metrics_ref)
    base = spectral_bound * (fa + fc) + penalty_weight
    raw = [table_row(table_ref, k) for k in range(6)]
    index = [jnp.maximum(r, 0) for r in raw]
    valid = [r >= 0 for r in raw]
    rows = row_ids()

    def pair_step(pair, carry):
        tiles = [[source.tile(2 * pair + h, t) for t in range(11)] for h in range(2)]
        zero = jnp.zeros((8, LANES), jnp.float32)
        both = jnp.concatenate(
            [jnp.concatenate(tiles[h] + [zero], axis=0) for h in range(2)], axis=1
        )
        high, low = split_value(both)
        ah, al = ah_ref[...], al_ref[...]
        second = mul(ah, high) + (mul(ah, low) + mul(al, high))
        low_main = low_ref[part, pl.ds(pl.multiple_of(8 * pair, 8), 8), :]
        top_main = top_ref[part, pl.ds(pl.multiple_of(8 * pair, 8), 8), :]
        low_rest = jnp.broadcast_to(low_ref[part, pl.ds(8 * pairs + pair, 1), :], (8, LANES))
        top_rest = jnp.broadcast_to(top_ref[part, pl.ds(8 * pairs + pair, 1), :], (8, LANES))
        for h in range(2):
            x = tiles[h]
            field = 2 * pair + h
            shift = shift_ref[start + field]
            scale = relaxation / (base + shift)
            low_index = index[4] + 64 * h
            top_index = index[5] + 64 * h

            def bottom(source, halo):
                own = jnp.where(valid[0], lane_take(source, index[0]), 0.0)
                return jnp.where(valid[4], lane_take(halo, low_index), own)

            def top(source, halo):
                own = jnp.where(valid[2], lane_take(source, index[2]), 0.0)
                return jnp.where(valid[5], lane_take(halo, top_index), own)

            for t in range(11):
                near = zero
                if t > 0 and t != 9:
                    right = jnp.where(valid[1], lane_take(x[t - 1], index[1]), 0.0)
                    near = near + jnp.where((rows + 8 * t) % 9 == 8, right, 0.0)
                if t < 8 or t == 9:
                    left = jnp.where(valid[3], lane_take(x[t + 1], index[3]), 0.0)
                    near = near + jnp.where((rows + 8 * t) % 9 == 0, left, 0.0)
                if t == 0:
                    near = near + bottom(x[9], low_main)
                if t == 1:
                    near = near + jnp.where(rows == 0, bottom(x[10], low_rest), 0.0)
                if t == 9:
                    near = near + top(x[0], top_main)
                if t == 10:
                    near = near + jnp.where(rows == 0, top(x[1], top_rest), 0.0)
                lanes = slice(LANES * h, LANES * h + LANES)
                lap = (
                    fa * second[8 * t : 8 * t + 8, lanes]
                    + fb * second[88 + 8 * t : 96 + 8 * t, lanes]
                    + fc * second[176 + 8 * t : 184 + 8 * t, lanes]
                )
                count = diag_ref[8 * t : 8 * t + 8, :]
                applied = shift * x[t] - lap + penalty_weight * (count * x[t] - near)
                finish(field, t, x[t], applied, scale)
        return carry

    lax.fori_loop(0, pairs, pair_step, 0)


def first_sweep(fields, operator, source, part, low_ref, top_ref, target):
    def finish(field, tile, x, applied, scale):
        target.put(field, tile, x + scale * (helm_shift * x - applied))

    apply_operator(fields, operator, source, part, low_ref, top_ref, finish)


def first_kernel(fields, *refs):
    operator, (x_ref, low_ref, top_ref, out_ref) = refs[:6], refs[6:]
    source, target = Field(x_ref, 0, fields), Field(out_ref, 0)
    first_sweep(fields, operator, source, 0, low_ref, top_ref, target)


def last_kernel(fields, *refs):
    operator = refs[:6]
    x_ref, low_ref, top_ref, vel_ref, adv_ref, out_ref, copy_ref = refs[6:]
    velocity, advection = Field(vel_ref, 0, fields), Field(adv_ref, 0)
    target, copied = Field(out_ref, 0, fields), Field(copy_ref, 0, fields)

    def finish(field, tile, x, applied, scale):
        term = advection.tile(field, tile)
        copied.put(field, tile, term)
        right = helm_shift * (velocity.tile(field, tile) - time_step * term)
        target.put(field, tile, x + scale * (right - applied))

    apply_operator(fields, operator, Field(x_ref, 0), 0, low_ref, top_ref, finish)


def state_kernel(
    fields, shift_ref, metrics_ref, table_ref, adv_ref, part_ref, state_ref, down_ref, up_ref
):
    start = lax.axis_index("modes") * fields
    fa, _, fc = factor_rows(metrics_ref)
    base = spectral_bound * (fa + fc) + penalty_weight
    advection, kept, state = Field(adv_ref, 0), Field(part_ref, 0), Field(state_ref, 0)
    for field in range(fields):
        weight = relaxation * helm_shift * time_step / (base + shift_ref[start + field])
        for tile in range(11):
            value = kept.tile(field, tile) - weight * advection.tile(field, tile)
            state.put(field, tile, value)
    emit_halo(state, table_ref, down_ref, up_ref, 0, fields)


def fused_kernel(
    mesh_count,
    shift_ref,
    metrics_ref,
    table_ref,
    ah_ref,
    al_ref,
    diag_ref,
    scalar_ref,
    bh_ref,
    bl_ref,
    dh_ref,
    dl_ref,
    ih_ref,
    il_ref,
    x_ref,
    state_ref,
    adv_ref,
    low2_ref,
    top2_ref,
    send,
    recv,
    back_send,
    back_recv,
    y0,
    y1,
    y2,
    part_ref,
    down_ref,
    up_ref,
    low_ref,
    top_ref,
    down2_ref,
    up2_ref,
    send_sem,
    recv_sem,
    back_send_sem,
    back_recv_sem,
    halo_send_sem,
    halo_recv_sem,
):
    fields, share = 16, 8
    operator = (shift_ref, metrics_ref, table_ref, ah_ref, al_ref, diag_ref)
    me = lax.axis_index("modes")
    row = lax.axis_index("mesh")
    above = lax.rem(row + 1, mesh_count)
    below = lax.rem(row + mesh_count - 1, mesh_count)
    peers = [lax.rem(me + k, 8) for k in range(8)]
    offset = me * 16
    stages = (y0, y1, y2)
    rows_ref = (below, above) if mesh_count > 1 else ()

    barrier = pltpu.get_barrier_semaphore()
    for k in range(1, 8):
        pl.semaphore_signal(barrier, inc=1, device_id=(row, peers[k]), device_id_type=MESH)
    for other in rows_ref:
        pl.semaphore_signal(barrier, inc=1, device_id=(other, me), device_id_type=MESH)

    def outgoing(half, f, k):
        return pltpu.make_async_remote_copy(
            src_ref=send.at[half, peers[k], pl.ds(88 * f, 88)],
            dst_ref=recv.at[half, me, pl.ds(88 * f, 88)],
            send_sem=send_sem.at[half, f, k],
            recv_sem=recv_sem.at[half, f, k],
            device_id=(row, peers[k]),
            device_id_type=MESH,
        )

    def returning(half, k):
        return pltpu.make_async_remote_copy(
            src_ref=back_send.at[half, peers[k]],
            dst_ref=back_recv.at[half, me],
            send_sem=back_send_sem.at[half, k],
            recv_sem=back_recv_sem.at[half, k],
            device_id=(row, peers[k]),
            device_id_type=MESH,
        )

    def halo_copies(phase, down, up, low, top):
        if mesh_count == 1:
            return []
        return [
            pltpu.make_async_remote_copy(
                src_ref=source,
                dst_ref=target,
                send_sem=halo_send_sem.at[phase, way],
                recv_sem=halo_recv_sem.at[phase, way],
                device_id=(other, me),
                device_id_type=MESH,
            )
            for way, source, target, other in ((0, up, low, above), (1, down, top, below))
        ]

    if mesh_count == 1:
        for ref in (low_ref, top_ref, low2_ref, top2_ref):
            ref[...] = jnp.zeros_like(ref)

    for f in range(3):
        source = Field(x_ref, f, fields)
        for tile in range(11):
            planes = swap_groups([source.tile(c, tile) for c in range(16)])
            first = 88 * f + 8 * tile
            for g in range(16):
                send[g % 2, g // 2, first : first + 8, :] = planes[g]
        if f == 0:
            pl.semaphore_wait(barrier, 7 + len(rows_ref))
        for k in range(1, 8):
            outgoing(0, f, k).start()
    for f in range(3):
        for k in range(1, 8):
            outgoing(1, f, k).start()
    for half in range(2):
        recv[half, me] = send[half, me]
    for f in range(3):
        emit_halo(Field(x_ref, f, fields), table_ref, down_ref, up_ref, f, fields)
    first_halo = halo_copies(0, down_ref, up_ref, low_ref, top_ref)
    for copy in first_halo:
        copy.start()

    for half in range(2):
        for f in range(3):
            for k in range(1, 8):
                outgoing(half, f, k).wait_recv()

        def spread(source, carry):
            for f in range(3):
                part = recv[half, source, 88 * f : 88 * f + 88, :]
                full = jnp.concatenate([part, jnp.zeros((40, LANES), jnp.float32)], axis=0)
                stages[f][pl.ds(pl.multiple_of(source * 128, 128), 128), :] = full.T
            return carry

        lax.fori_loop(0, 8, spread, 0)

        def element(e, carry):
            value = jnp.concatenate(
                [stages[f][pl.ds(e, 128, stride=share), :] for f in range(3)], axis=1
            )
            high, low = split_value(value)
            planes = mul(bh_ref[...], jnp.concatenate([high, low], axis=0)) + mul(
                bl_ref[...], high
            )
            u, v, w = (planes[:128, 128 * f : 128 * f + 128] for f in range(3))
            high, low = split_value(jnp.concatenate([u, v, w], axis=0))
            grads = mul(jnp.concatenate([high, low], axis=1), dh_ref[...]) + mul(
                high, dl_ref[...]
            )
            rx, ry, sx, sy = (scalar_ref[k, offset + share * half + e] for k in range(4))
            along_r = rx * u + ry * v
            along_s = sx * u + sy * v
            terms = []
            for f in range(3):
                rows = slice(128 * f, 128 * f + 128)
                terms.append(
                    along_r * grads[rows, :128]
                    + along_s * grads[rows, 128:]
                    + w * planes[128:, 128 * f : 128 * f + 128]
                )
            high, low = split_value(jnp.concatenate(terms, axis=1))
            back = mul(ih_ref[...], jnp.concatenate([high, low], axis=0)) + mul(
                il_ref[...], high
            )
            for f in range(3):
                stages[f][pl.ds(e, 128, stride=share), :] = back[:, 128 * f : 128 * f + 128]
            return carry

        lax.fori_loop(0, share, element, 0)

        def collect(target, carry):
            for f in range(3):
                full = stages[f][pl.ds(pl.multiple_of(target * 128, 128), 128), :]
                back_send[half, target, 88 * f : 88 * f + 88, :] = full.T[:88, :]
            return carry

        lax.fori_loop(0, 8, collect, 0)
        for k in range(1, 8):
            returning(half, k).start()
        back_recv[half, me] = back_send[half, me]

    for copy in first_halo:
        copy.wait()
    for f in range(3):
        first_sweep(
            fields, operator, Field(x_ref, f, fields), f, low_ref, top_ref, Field(part_ref, f)
        )

    for half in range(2):
        for k in range(1, 8):
            returning(half, k).wait_recv()
    fa, _, fc = factor_rows(metrics_ref)
    base = spectral_bound * (fa + fc) + penalty_weight
    for f in range(3):
        advection, kept, state = Field(adv_ref, f), Field(part_ref, f), Field(state_ref, f)
        for tile in range(11):
            first = 88 * f + 8 * tile
            planes = swap_groups(
                [back_recv[g % 2, g // 2, first : first + 8, :] for g in range(16)]
            )
            for c in range(16):
                advection.put(c, tile, planes[c])
        for c in range(16):
            weight = relaxation * helm_shift * time_step / (base + shift_ref[me * 16 + c])
            for tile in range(11):
                value = kept.tile(c, tile) - weight * advection.tile(c, tile)
                state.put(c, tile, value)
        emit_halo(state, table_ref, down2_ref, up2_ref, f, fields)
    second_halo = halo_copies(1, down2_ref, up2_ref, low2_ref, top2_ref)
    for copy in second_halo:
        copy.start()
    for half in range(2):
        for k in range(1, 8):
            for f in range(3):
                outgoing(half, f, k).wait_send()
            returning(half, k).wait_send()
    for copy in second_halo:
        copy.wait()


def plain_advection(velocity, metrics, tables, mode_count):
    along_r, along_s, basis, inverse, plane_z = tables
    share = velocity.shape[3] // mode_count
    mode_index = lax.axis_index("modes")
    local = lax.dynamic_slice_in_dim(metrics, mode_index * share, share, axis=1)
    field = lax.all_to_all(velocity, "modes", split_axis=3, concat_axis=1, tiled=True)
    physical = jnp.einsum("pc,fcqe->fpqe", basis, field, precision=highest)
    grad_z = jnp.einsum("pc,fcqe->fpqe", plane_z, field, precision=highest)
    grad_r = jnp.einsum("qr,fpre->fpqe", along_r, physical, precision=highest)
    grad_s = jnp.einsum("qr,fpre->fpqe", along_s, physical, precision=highest)
    grad_x = local[0] * grad_r + local[2] * grad_s
    grad_y = local[1] * grad_r + local[3] * grad_s
    term = physical[0] * grad_x + physical[1] * grad_y + physical[2] * grad_z
    spectral = jnp.einsum("cp,fpqe->fcqe", inverse, term, precision=highest)
    return lax.all_to_all(spectral, "modes", split_axis=1, concat_axis=3, tiled=True)


def body(velocity, metrics, connect, send_list, recv_slot):
    along_r, along_s, second, counts, basis, inverse, z_derivative, shifts = spectral_tables(COEF)
    mode_count = lax.axis_size("modes")
    mesh_index = lax.axis_index("mesh")
    fields = velocity.shape[1]
    elements = velocity.shape[3]
    packed = mode_count == 8
    own = jnp.where(
        connect < 0, -1, jnp.clip(connect - mesh_index * elements, 0, elements - 1)
    )
    table = jnp.concatenate(
        [own.T, recv_slot.T, jnp.concatenate([send_list, send_list], axis=1)], axis=0
    )
    shifts = jnp.asarray(shifts, jnp.float32)
    halo_rows = 8 * (fields // 2) + (fields // 2 + 7) // 8 * 8
    ah, al = split_table(
        np.concatenate([pad_table(second[k], 88, 96) for k in range(3)], axis=0)
    )
    diag = np.zeros((88, LANES), np.float32)
    diag[:81] = counts[:, None]

    field_shape = jax.ShapeDtypeStruct(velocity.shape, jnp.float32)
    halo_shape = jax.ShapeDtypeStruct((3, halo_rows, LANES), jnp.float32)
    native = velocity.transpose(0, 2, 1, 3).reshape(3, 81 * fields, LANES)
    native_shape = jax.ShapeDtypeStruct(native.shape, jnp.float32)
    native_spec = pl.BlockSpec((1, 81 * fields, LANES), lambda f: (f, 0, 0))
    field_spec = pl.BlockSpec((1, fields, 81, LANES), lambda f: (f, 0, 0, 0))
    halo_spec = pl.BlockSpec((1, halo_rows, LANES), lambda f: (f, 0, 0))
    smem = pl.BlockSpec(memory_space=pltpu.SMEM)

    def whole(shape):
        return pl.BlockSpec(shape, lambda f: (0,) * len(shape))

    params = pltpu.CompilerParams(vmem_limit_bytes=48 << 20)
    metric_spec, table_spec = whole((4, LANES)), whole((8, LANES))
    operator_specs = [
        smem,
        metric_spec,
        table_spec,
        whole((264, 96)),
        whole((264, 96)),
        whole((88, LANES)),
    ]
    operator_tables = (shifts, metrics, table, jnp.asarray(ah), jnp.asarray(al), jnp.asarray(diag))

    plane_z = basis @ z_derivative
    if packed:
        bh, bl = split_table(np.concatenate([basis, plane_z], axis=0))
        dh, dl = split_table(
            np.concatenate(
                [pad_table(along_r.T, 128, 128), pad_table(along_s.T, 128, 128)], axis=1
            )
        )
        ih, il = split_table(inverse)
        vmem = pl.BlockSpec(memory_space=pltpu.VMEM)
        halo_buffer = pltpu.VMEM((3, halo_rows, LANES), jnp.float32)
        trade_buffer = pltpu.VMEM((2, 8, 264, LANES), jnp.float32)
        state, advection, low, top = pl.pallas_call(
            functools.partial(fused_kernel, lax.axis_size("mesh")),
            in_specs=[smem] + [vmem] * 5 + [smem] + [vmem] * 7,
            out_specs=[vmem] * 4,
            out_shape=[field_shape, field_shape, halo_shape, halo_shape],
            scratch_shapes=[trade_buffer] * 4
            + [pltpu.VMEM((1024, LANES), jnp.float32)] * 3
            + [pltpu.VMEM(velocity.shape, jnp.float32)]
            + [halo_buffer] * 6
            + [pltpu.SemaphoreType.DMA((2, 3, 8))] * 2
            + [pltpu.SemaphoreType.DMA((2, 8))] * 2
            + [pltpu.SemaphoreType.DMA((2, 2))] * 2,
            compiler_params=pltpu.CompilerParams(
                vmem_limit_bytes=48 << 20, collective_id=0, has_side_effects=True
            ),
        )(
            *operator_tables,
            metrics,
            jnp.asarray(np.concatenate([bh, bh], axis=1)),
            jnp.asarray(bl),
            jnp.asarray(np.concatenate([dh, dh], axis=0)),
            jnp.asarray(dl),
            jnp.asarray(np.concatenate([ih, ih], axis=1)),
            jnp.asarray(il),
            native,
        )
    else:
        tables = [
            jnp.asarray(t, jnp.float32) for t in (along_r, along_s, basis, inverse, plane_z)
        ]
        advection = plain_advection(velocity, metrics, tables, mode_count)
        down, up = pl.pallas_call(
            functools.partial(halo_kernel, fields),
            grid=(3,),
            in_specs=[table_spec, native_spec],
            out_specs=[halo_spec, halo_spec],
            out_shape=[halo_shape, halo_shape],
            compiler_params=params,
        )(table, native)
        part = pl.pallas_call(
            functools.partial(first_kernel, fields),
            grid=(3,),
            in_specs=operator_specs + [native_spec, halo_spec, halo_spec],
            out_specs=field_spec,
            out_shape=field_shape,
            compiler_params=params,
        )(*operator_tables, native, shifted(up, "mesh", 1), shifted(down, "mesh", -1))
        state, down, up = pl.pallas_call(
            functools.partial(state_kernel, fields),
            grid=(3,),
            in_specs=[smem, metric_spec, table_spec, field_spec, field_spec],
            out_specs=[field_spec, halo_spec, halo_spec],
            out_shape=[field_shape, halo_shape, halo_shape],
            compiler_params=params,
        )(shifts, metrics, table, advection, part)
        low = shifted(up, "mesh", 1)
        top = shifted(down, "mesh", -1)

    results = pl.pallas_call(
        functools.partial(last_kernel, fields),
        grid=(3,),
        in_specs=operator_specs + [field_spec, halo_spec, halo_spec, native_spec, field_spec],
        out_specs=[native_spec, native_spec],
        out_shape=[native_shape, native_shape],
        compiler_params=params,
    )(*operator_tables, state, low, top, native, advection)
    return tuple(
        out.reshape(3, 81, fields, LANES).transpose(0, 2, 1, 3) for out in results
    )


def solution(mesh):
    return jax.shard_map(
        body,
        mesh=mesh,
        in_specs=(
            P(None, "modes", None, "mesh"),
            P(None, "mesh"),
            P("mesh", None),
            P("mesh", None),
            P("mesh", None),
        ),
        out_specs=(P(None, "modes", None, "mesh"), P(None, "modes", None, "mesh")),
        check_vma=False,
    )
```

time: 125 us -> 92.2 us (0.74)
  the two profiles are of different devices: /device:TPU:0 before, /device:TPU:1 now
where the time goes in v2:
time: 92.2 us; the launch traced here: 91.6 us
  Pallas kernels  78.9 us (86%)
  local copies, waits for them, and re-layouts  10.5 us (11%)
  other arithmetic  1.52 us (2%)
    pallas_call x1, Pallas kernels, body(): pl.pallas_call(functools.partial(fused_kernel, lax.axis_size('mesh')), in...  68.8 us
    unnamed x26, local copies, waits for them, and re-layouts  10.5 us
    pallas_call x1, Pallas kernels, body(): pl.pallas_call(functools.partial(last_kernel, fields), grid=(3,), in_spec...  10.1 us

profile of v2, /device:TPU:1, one launch (start us, length us, event | category | flops | bytes accessed | tf_op | source)
XLA Modules:
  0.0 91.6 jit_solution(4400262310758038489)
XLA Ops:
  0.6 0.7 select_bitcast_fusion
  1.3 0.8 add_add_fusion.table_ref.refs_2_
  2.2 0.0 copy-start
  2.2 1.6 %copy-done = f32[3,16,81,128]{3,1,2,0:T(8,128)S(1)} copy-done((f32[3,16,81,128]{3,1,2,0:T(8,128)S(1)}, f32[3,16,81,128]{3,1,2,0:T(8,128)}, u32[]{:S(2)}) %copy-start) | copy-done | bytes 1990680
  3.7 0.0 copy-start.2
  3.7 0.9 copy-done.2
  4.6 0.0 copy-start.3
  4.6 0.9 copy-done.3
  5.5 0.0 copy-start.4
  5.5 0.8 copy-done.4
  6.3 0.0 copy-start.5
  6.3 0.9 copy-done.5
  7.2 0.0 copy-start.6
  7.2 0.9 copy-done.6
  8.1 0.0 copy-start.7
  8.1 0.8 copy-done.7
  8.9 0.0 copy-start.8
  8.9 0.8 copy-done.8
  9.8 0.0 copy-start.9
  9.8 0.8 copy-done.9
  10.6 0.0 copy-start.10
  10.6 0.8 copy-done.10
  11.4 0.0 copy-start.11
  11.4 0.7 copy-done.11
  12.0 0.0 copy-start.12
  12.0 0.7 copy-done.12
  12.7 0.0 copy-start.1
  12.7 68.8 %shard_map.158 = (f32[3,16,81,128]{3,2,1,0:T(8,128)S(1)}, f32[3,16,81,128]{3,2,1,0:T(8,128)}, f32[3,72,128]{2,1,0:T(8,128)S(1)}, f32[3,72,128]{2,1,0:T(8,128)S(1)}) custom-call(f32[128]{0:T(128)S(1)} %copy-done.12, f32[4,128]{1,0:T(4,128)S(1)} %copy-done.11, s32[8,128]{1,0:T(8,128)S(1)} %add_add_fusion.table_ref.refs_2_, bf16[264,96]{1,0:T(8,128)(2,1)S(1)} %copy-done.3, ...), custom_call_target="tpu_custom_call" | custom-call | tf_op jit(solution)/shard_map/pallas_call | solution.py:627
  81.5 0.0 copy-done.1
  81.5 10.1 %shard_map.159 = (f32[3,1296,128]{2,1,0:T(8,128)}, f32[3,1296,128]{2,1,0:T(8,128)}) custom-call(f32[128]{0:T(128)S(1)} %copy-done.12, f32[4,128]{1,0:T(4,128)S(1)} %copy-done.11, s32[8,128]{1,0:T(8,128)S(1)} %add_add_fusion.table_ref.refs_2_, bf16[264,96]{1,0:T(8,128)(2,1)S(1)} %copy-done.3, bf16[264,96]{1,0:T(8,128)(2,1)S(1)} %copy-done.2, ...), custom_call_target="tpu_custom_call" | custom-call | tf_op jit(solution)/shard_map/pallas_call | solution.py:685
Async XLA Ops:
  2.2 1.6 %copy-start = (f32[3,16,81,128]{3,1,2,0:T(8,128)S(1)}, f32[3,16,81,128]{3,1,2,0:T(8,128)}, u32[]{:S(2)}) copy-start(f32[3,16,81,128]{3,1,2,0:T(8,128)} %param.15) | copy-start | bytes 5971972
  3.7 0.9 copy-start.2
  4.6 0.9 copy-start.3
  5.5 0.8 copy-start.4
  6.3 0.9 copy-start.5
  7.2 0.9 copy-start.6
  8.1 0.8 copy-start.7
  8.9 0.8 copy-start.8
  9.8 0.8 copy-start.9
  10.6 0.8 copy-start.10
  11.4 0.7 copy-start.11
  12.0 0.7 copy-start.12
  12.7 68.8 %copy-start.1 = (f32[3,16,81,128]{3,1,2,0:T(8,128)S(1)}, f32[3,16,81,128]{3,1,2,0:T(8,128)}, u32[]{:S(2)}) copy-start(f32[3,16,81,128]{3,1,2,0:T(8,128)} %param.15) | copy-start | bytes 5971972

commit v3 on v2

--- a/solution.py
+++ b/solution.py
@@ -185,6 +185,11 @@
                 continue
             j = i | bit
             first, second = planes[i], planes[j]
+            if bit == 8:
+                moved = pltpu.roll(jnp.where(upper, first, second), 64, 1)
+                planes[i] = jnp.where(upper, moved, first)
+                planes[j] = jnp.where(upper, second, moved)
+                continue
             planes[i] = jnp.where(upper, pltpu.roll(second, 8 * bit, 1), first)
             planes[j] = jnp.where(upper, second, pltpu.roll(first, LANES - 8 * bit, 1))
     return planes
@@ -221,7 +226,7 @@
 
 
 def apply_operator(fields, operator, source, part, low_ref, top_ref, finish):
-    shift_ref, metrics_ref, table_ref, ah_ref, al_ref, diag_ref = operator
+    shift_ref, metrics_ref, table_ref, diag_ref, load_second = operator
     pairs = fields // 2
     start = lax.axis_index("modes") * fields
     fa, fb, fc = factor_rows(metrics_ref)
@@ -238,7 +243,7 @@
             [jnp.concatenate(tiles[h] + [zero], axis=0) for h in range(2)], axis=1
         )
         high, low = split_value(both)
-        ah, al = ah_ref[...], al_ref[...]
+        ah, al = load_second()
         second = mul(ah, high) + (mul(ah, low) + mul(al, high))
         low_main = low_ref[part, pl.ds(pl.multiple_of(8 * pair, 8), 8), :]
         top_main = top_ref[part, pl.ds(pl.multiple_of(8 * pair, 8), 8), :]
@@ -264,10 +269,10 @@
                 near = zero
                 if t > 0 and t != 9:
                     right = jnp.where(valid[1], lane_take(x[t - 1], index[1]), 0.0)
-                    near = near + jnp.where((rows + 8 * t) % 9 == 8, right, 0.0)
+                    near = near + jnp.where(rows == (8 - 8 * t) % 9, right, 0.0)
                 if t < 8 or t == 9:
                     left = jnp.where(valid[3], lane_take(x[t + 1], index[3]), 0.0)
-                    near = near + jnp.where((rows + 8 * t) % 9 == 0, left, 0.0)
+                    near = near + jnp.where(rows == -8 * t % 9, left, 0.0)
                 if t == 0:
                     near = near + bottom(x[9], low_main)
                 if t == 1:
@@ -283,11 +288,11 @@
                     + fc * second[176 + 8 * t : 184 + 8 * t, lanes]
                 )
                 count = diag_ref[8 * t : 8 * t + 8, :]
-                applied = shift * x[t] - lap + penalty_weight * (count * x[t] - near)
+                applied = (shift + count) * x[t] - lap - penalty_weight * near
                 finish(field, t, x[t], applied, scale)
         return carry
 
-    lax.fori_loop(0, pairs, pair_step, 0)
+    lax.fori_loop(0, pairs, pair_step, 0, unroll=2)
 
 
 def first_sweep(fields, operator, source, part, low_ref, top_ref, target):
@@ -297,14 +302,19 @@
     apply_operator(fields, operator, source, part, low_ref, top_ref, finish)
 
 
+def operator_of(refs):
+    shift_ref, metrics_ref, table_ref, ah_ref, al_ref, diag_ref = refs
+    return shift_ref, metrics_ref, table_ref, diag_ref, lambda: (ah_ref[...], al_ref[...])
+
+
 def first_kernel(fields, *refs):
-    operator, (x_ref, low_ref, top_ref, out_ref) = refs[:6], refs[6:]
+    operator, (x_ref, low_ref, top_ref, out_ref) = operator_of(refs[:6]), refs[6:]
     source, target = Field(x_ref, 0, fields), Field(out_ref, 0)
     first_sweep(fields, operator, source, 0, low_ref, top_ref, target)
 
 
 def last_kernel(fields, *refs):
-    operator = refs[:6]
+    operator = operator_of(refs[:6])
     x_ref, low_ref, top_ref, vel_ref, adv_ref, out_ref, copy_ref = refs[6:]
     velocity, advection = Field(vel_ref, 0, fields), Field(adv_ref, 0)
     target, copied = Field(out_ref, 0, fields), Field(copy_ref, 0, fields)
@@ -336,23 +346,26 @@
 def fused_kernel(
     mesh_count,
     shift_ref,
-    metrics_ref,
-    table_ref,
-    ah_ref,
-    al_ref,
-    diag_ref,
     scalar_ref,
-    bh_ref,
-    bl_ref,
-    dh_ref,
-    dl_ref,
-    ih_ref,
-    il_ref,
-    x_ref,
+    metrics_in,
+    connect_in,
+    slot_in,
+    list_in,
+    diag_in,
+    constants_in,
+    x_in,
     state_ref,
     adv_ref,
     low2_ref,
     top2_ref,
+    table_ref,
+    metrics_ref,
+    connect_ref,
+    slot_ref,
+    list_ref,
+    diag_ref,
+    constants,
+    x_ref,
     send,
     recv,
     back_send,
@@ -360,6 +373,9 @@
     y0,
     y1,
     y2,
+    z0,
+    z1,
+    z2,
     part_ref,
     down_ref,
     up_ref,
@@ -373,16 +389,41 @@
     back_recv_sem,
     halo_send_sem,
     halo_recv_sem,
+    load_sem,
 ):
     fields, share = 16, 8
-    operator = (shift_ref, metrics_ref, table_ref, ah_ref, al_ref, diag_ref)
+    operator = (
+        shift_ref,
+        metrics_ref,
+        table_ref,
+        diag_ref,
+        lambda: (constants[1024:1288, 0:96], constants[1024:1288, 128:224]),
+    )
+    x_loads = [
+        pltpu.make_async_copy(x_in.at[f], x_ref.at[f], load_sem.at[f]) for f in range(3)
+    ]
+    loads = [
+        pltpu.make_async_copy(source, target, load_sem.at[3 + i])
+        for i, (source, target) in enumerate(
+            (
+                (connect_in, connect_ref),
+                (slot_in, slot_ref),
+                (list_in, list_ref),
+                (metrics_in, metrics_ref),
+                (diag_in, diag_ref),
+                (constants_in, constants),
+            )
+        )
+    ]
+    for copy in x_loads + loads:
+        copy.start()
     me = lax.axis_index("modes")
     row = lax.axis_index("mesh")
     above = lax.rem(row + 1, mesh_count)
     below = lax.rem(row + mesh_count - 1, mesh_count)
     peers = [lax.rem(me + k, 8) for k in range(8)]
     offset = me * 16
-    stages = (y0, y1, y2)
+    stages, results = (y0, y1, y2), (z0, z1, z2)
     rows_ref = (below, above) if mesh_count > 1 else ()
 
     barrier = pltpu.get_barrier_semaphore()
@@ -432,6 +473,7 @@
 
     for f in range(3):
         source = Field(x_ref, f, fields)
+        x_loads[f].wait()
         for tile in range(11):
             planes = swap_groups([source.tile(c, tile) for c in range(16)])
             first = 88 * f + 8 * tile
@@ -441,16 +483,32 @@
             pl.semaphore_wait(barrier, 7 + len(rows_ref))
         for k in range(1, 8):
             outgoing(0, f, k).start()
-    for f in range(3):
-        for k in range(1, 8):
-            outgoing(1, f, k).start()
-    for half in range(2):
-        recv[half, me] = send[half, me]
+    for copy in loads:
+        copy.wait()
+    elements = connect_ref.shape[1]
+    local = jnp.clip(connect_ref[...] - row * elements, 0, elements - 1)
+    table_ref[0:4, :] = jnp.where(connect_ref[...] < 0, -1, local)
+    table_ref[4:6, :] = slot_ref[...]
+    table_ref[6:8, :] = jnp.concatenate([list_ref[...], list_ref[...]], axis=1)
     for f in range(3):
         emit_halo(Field(x_ref, f, fields), table_ref, down_ref, up_ref, f, fields)
     first_halo = halo_copies(0, down_ref, up_ref, low_ref, top_ref)
     for copy in first_halo:
         copy.start()
+    for half in range(2):
+        recv[half, me] = send[half, me]
+    for f in range(3):
+        for k in range(1, 8):
+            outgoing(1, f, k).start()
+
+    def sweep(f):
+        first_sweep(
+            fields, operator, Field(x_ref, f, fields), f, low_ref, top_ref, Field(part_ref, f)
+        )
+
+    for copy in first_halo:
+        copy.wait()
+    sweep(0)
 
     for half in range(2):
         for f in range(3):
@@ -464,59 +522,61 @@
                 stages[f][pl.ds(pl.multiple_of(source * 128, 128), 128), :] = full.T
             return carry
 
-        lax.fori_loop(0, 8, spread, 0)
-
-        def element(e, carry):
+        lax.fori_loop(0, 8, spread, 0, unroll=2)
+
+        def element(step, carry):
+            picks = (2 * step, 2 * step + 1)
             value = jnp.concatenate(
-                [stages[f][pl.ds(e, 128, stride=share), :] for f in range(3)], axis=1
+                [stages[f][pl.ds(e, 128, stride=share), :] for e in picks for f in range(3)],
+                axis=1,
             )
             high, low = split_value(value)
-            planes = mul(bh_ref[...], jnp.concatenate([high, low], axis=0)) + mul(
-                bl_ref[...], high
-            )
-            u, v, w = (planes[:128, 128 * f : 128 * f + 128] for f in range(3))
-            high, low = split_value(jnp.concatenate([u, v, w], axis=0))
-            grads = mul(jnp.concatenate([high, low], axis=1), dh_ref[...]) + mul(
-                high, dl_ref[...]
-            )
-            rx, ry, sx, sy = (scalar_ref[k, offset + share * half + e] for k in range(4))
-            along_r = rx * u + ry * v
-            along_s = sx * u + sy * v
+            planes = mul(constants[0:256, :], jnp.concatenate([high, low], axis=0)) + mul(
+                constants[768:1024, 0:128], high
+            )
+            parts = [planes[:128, 128 * f : 128 * f + 128] for f in range(6)]
+            high, low = split_value(jnp.concatenate(parts, axis=0))
+            grads = mul(jnp.concatenate([high, low], axis=1), constants[256:512, :]) + mul(
+                high, constants[640:768, :]
+            )
             terms = []
-            for f in range(3):
-                rows = slice(128 * f, 128 * f + 128)
-                terms.append(
-                    along_r * grads[rows, :128]
-                    + along_s * grads[rows, 128:]
-                    + w * planes[128:, 128 * f : 128 * f + 128]
-                )
+            for i, e in enumerate(picks):
+                u, v, w = parts[3 * i : 3 * i + 3]
+                rx, ry, sx, sy = (scalar_ref[k, offset + share * half + e] for k in range(4))
+                along_r = rx * u + ry * v
+                along_s = sx * u + sy * v
+                for f in range(3 * i, 3 * i + 3):
+                    rows = slice(128 * f, 128 * f + 128)
+                    terms.append(
+                        along_r * grads[rows, :128]
+                        + along_s * grads[rows, 128:]
+                        + w * planes[128:, 128 * f : 128 * f + 128]
+                    )
             high, low = split_value(jnp.concatenate(terms, axis=1))
-            back = mul(ih_ref[...], jnp.concatenate([high, low], axis=0)) + mul(
-                il_ref[...], high
-            )
-            for f in range(3):
-                stages[f][pl.ds(e, 128, stride=share), :] = back[:, 128 * f : 128 * f + 128]
+            back = mul(constants[512:640, :], jnp.concatenate([high, low], axis=0)) + mul(
+                constants[768:896, 128:256], high
+            )
+            for i, e in enumerate(picks):
+                for f in range(3):
+                    first = 128 * (3 * i + f)
+                    results[f][pl.ds(e, 128, stride=share), :] = back[:, first : first + 128]
             return carry
 
-        lax.fori_loop(0, share, element, 0)
+        lax.fori_loop(0, share // 2, element, 0, unroll=2)
 
         def collect(target, carry):
             for f in range(3):
-                full = stages[f][pl.ds(pl.multiple_of(target * 128, 128), 128), :]
+                full = results[f][pl.ds(pl.multiple_of(target * 128, 128), 128), :]
                 back_send[half, target, 88 * f : 88 * f + 88, :] = full.T[:88, :]
             return carry
 
-        lax.fori_loop(0, 8, collect, 0)
+        lax.fori_loop(0, 8, collect, 0, unroll=2)
         for k in range(1, 8):
             returning(half, k).start()
         back_recv[half, me] = back_send[half, me]
 
-    for copy in first_halo:
-        copy.wait()
-    for f in range(3):
-        first_sweep(
-            fields, operator, Field(x_ref, f, fields), f, low_ref, top_ref, Field(part_ref, f)
-        )
+    sweep(1)
+    sweep(2)
 
     for half in range(2):
         for k in range(1, 8):
@@ -574,19 +634,13 @@
     fields = velocity.shape[1]
     elements = velocity.shape[3]
     packed = mode_count == 8
-    own = jnp.where(
-        connect < 0, -1, jnp.clip(connect - mesh_index * elements, 0, elements - 1)
-    )
-    table = jnp.concatenate(
-        [own.T, recv_slot.T, jnp.concatenate([send_list, send_list], axis=1)], axis=0
-    )
     shifts = jnp.asarray(shifts, jnp.float32)
     halo_rows = 8 * (fields // 2) + (fields // 2 + 7) // 8 * 8
     ah, al = split_table(
         np.concatenate([pad_table(second[k], 88, 96) for k in range(3)], axis=0)
     )
     diag = np.zeros((88, LANES), np.float32)
-    diag[:81] = counts[:, None]
+    diag[:81] = penalty_weight * counts[:, None]
 
     field_shape = jax.ShapeDtypeStruct(velocity.shape, jnp.float32)
     halo_shape = jax.ShapeDtypeStruct((3, halo_rows, LANES), jnp.float32)
@@ -600,7 +654,7 @@
     def whole(shape):
         return pl.BlockSpec(shape, lambda f: (0,) * len(shape))
 
-    params = pltpu.CompilerParams(vmem_limit_bytes=48 << 20)
+    params = pltpu.CompilerParams(vmem_limit_bytes=60 << 20)
     metric_spec, table_spec = whole((4, LANES)), whole((8, LANES))
     operator_specs = [
         smem,
@@ -610,7 +664,7 @@
         whole((264, 96)),
         whole((88, LANES)),
     ]
-    operator_tables = (shifts, metrics, table, jnp.asarray(ah), jnp.asarray(al), jnp.asarray(diag))
+    ah_table, al_table, diag_table = (jnp.asarray(t) for t in (ah, al, diag))
 
     plane_z = basis @ z_derivative
     if packed:
@@ -621,36 +675,68 @@
             )
         )
         ih, il = split_table(inverse)
+        constants = np.zeros((1296, 256), ml_dtypes.bfloat16)
+        constants[0:256] = np.concatenate([bh, bh], axis=1)
+        constants[256:512] = np.concatenate([dh, dh], axis=0)
+        constants[512:640] = np.concatenate([ih, ih], axis=1)
+        constants[640:768] = dl
+        constants[768:1024, 0:128] = bl
+        constants[768:896, 128:256] = il
+        constants[1024:1288, 0:96] = ah
+        constants[1024:1288, 128:224] = al
         vmem = pl.BlockSpec(memory_space=pltpu.VMEM)
+        hbm = pl.BlockSpec(memory_space=pltpu.HBM)
         halo_buffer = pltpu.VMEM((3, halo_rows, LANES), jnp.float32)
         trade_buffer = pltpu.VMEM((2, 8, 264, LANES), jnp.float32)
-        state, advection, low, top = pl.pallas_call(
+        state, advection, low, top, table = pl.pallas_call(
             functools.partial(fused_kernel, lax.axis_size("mesh")),
-            in_specs=[smem] + [vmem] * 5 + [smem] + [vmem] * 7,
-            out_specs=[vmem] * 4,
-            out_shape=[field_shape, field_shape, halo_shape, halo_shape],
-            scratch_shapes=[trade_buffer] * 4
-            + [pltpu.VMEM((1024, LANES), jnp.float32)] * 3
+            in_specs=[smem] * 2 + [hbm] * 7,
+            out_specs=[vmem] * 5,
+            out_shape=[
+                field_shape,
+                field_shape,
+                halo_shape,
+                halo_shape,
+                jax.ShapeDtypeStruct((8, LANES), jnp.int32),
+            ],
+            scratch_shapes=[
+                pltpu.VMEM((4, LANES), jnp.float32),
+                pltpu.VMEM((4, LANES), jnp.int32),
+                pltpu.VMEM((2, LANES), jnp.int32),
+                pltpu.VMEM(send_list.shape, jnp.int32),
+                pltpu.VMEM(diag.shape, jnp.float32),
+                pltpu.VMEM(constants.shape, jnp.bfloat16),
+                pltpu.VMEM(native.shape, jnp.float32),
+            ]
+            + [trade_buffer] * 4
+            + [pltpu.VMEM((1024, LANES), jnp.float32)] * 6
             + [pltpu.VMEM(velocity.shape, jnp.float32)]
             + [halo_buffer] * 6
             + [pltpu.SemaphoreType.DMA((2, 3, 8))] * 2
             + [pltpu.SemaphoreType.DMA((2, 8))] * 2
-            + [pltpu.SemaphoreType.DMA((2, 2))] * 2,
+            + [pltpu.SemaphoreType.DMA((2, 2))] * 2
+            + [pltpu.SemaphoreType.DMA((9,))],
             compiler_params=pltpu.CompilerParams(
-                vmem_limit_bytes=48 << 20, collective_id=0, has_side_effects=True
+                vmem_limit_bytes=60 << 20, collective_id=0, has_side_effects=True
             ),
         )(
-            *operator_tables,
+            shifts,
             metrics,
-            jnp.asarray(np.concatenate([bh, bh], axis=1)),
-            jnp.asarray(bl),
-            jnp.asarray(np.concatenate([dh, dh], axis=0)),
-            jnp.asarray(dl),
-            jnp.asarray(np.concatenate([ih, ih], axis=1)),
-            jnp.asarray(il),
+            metrics,
+            connect.T,
+            recv_slot.T,
+            send_list,
+            jnp.asarray(diag),
+            jnp.asarray(constants),
             native,
         )
     else:
+        own = jnp.where(
+            connect < 0, -1, jnp.clip(connect - mesh_index * elements, 0, elements - 1)
+        )
+        table = jnp.concatenate(
+            [own.T, recv_slot.T, jnp.concatenate([send_list, send_list], axis=1)], axis=0
+        )
         tables = [
             jnp.asarray(t, jnp.float32) for t in (along_r, along_s, basis, inverse, plane_z)
         ]
@@ -670,7 +756,7 @@
             out_specs=field_spec,
             out_shape=field_shape,
             compiler_params=params,
-        )(*operator_tables, native, shifted(up, "mesh", 1), shifted(down, "mesh", -1))
+        )(shifts, metrics, table, ah_table, al_table, diag_table, native, shifted(up, "mesh", 1), shifted(down, "mesh", -1))
         state, down, up = pl.pallas_call(
             functools.partial(state_kernel, fields),
             grid=(3,),
@@ -689,7 +775,7 @@
         out_specs=[native_spec, native_spec],
         out_shape=[native_shape, native_shape],
         compiler_params=params,
-    )(*operator_tables, state, low, top, native, advection)
+    )(shifts, metrics, table, ah_table, al_table, diag_table, state, low, top, native, advection)
     return tuple(
         out.reshape(3, 81, fields, LANES).transpose(0, 2, 1, 3) for out in results
     )

time: 92.2 us -> 80.9 us (0.88)
  local copies, waits for them, and re-layouts: 10.5 us -> 0 us
  other arithmetic: 1.52 us -> 0 us
  Pallas kernels: 78.9 us -> 80.1 us
    unnamed x26 -> x0, local copies, waits for them, and re-layouts: 10.5 us -> none
    pallas_call x1, Pallas kernels: 68.8 us -> 70.7 us  [body(): pl.pallas_call(functools.partial(fused_kernel, lax.axis_size('mesh')), in...]
where the time goes in v3:
time: 80.9 us; the launch traced here: 80.7 us
  Pallas kernels  80.1 us (99%)
    pallas_call x1, Pallas kernels, body(): pl.pallas_call(functools.partial(fused_kernel, lax.axis_size('mesh')), in...  70.7 us
    pallas_call x1, Pallas kernels, body(): pl.pallas_call(functools.partial(last_kernel, fields), grid=(3,), in_spec...  9.37 us

profile of v3, /device:TPU:1, one launch (start us, length us, event | category | flops | bytes accessed | tf_op | source)
XLA Modules:
  0.0 80.7 jit_solution(11667786611706851813)
XLA Ops:
  0.6 70.7 %shard_map.113 = (f32[3,16,81,128]{3,2,1,0:T(8,128)}, f32[3,16,81,128]{3,2,1,0:T(8,128)}, f32[3,72,128]{2,1,0:T(8,128)}, f32[3,72,128]{2,1,0:T(8,128)}, s32[8,128]{1,0:T(8,128)}) custom-call(f32[128]{0:T(128)} %constant.10.clone.shift_ref.refs_0_, f32[4,128]{1,0:T(4,128)} %refs_1_.1, f32[4,128]{1,0:T(4,128)} %refs_1_.1, s32[4,128]{1,0:T(4,128)} %bitcast.13, ...), custom_call_target="tpu_custom_call" | custom-call | tf_op jit(solution)/shard_map/pallas_call | solution.py:691
  71.4 9.4 %shard_map.114 = (f32[3,1296,128]{2,1,0:T(8,128)}, f32[3,1296,128]{2,1,0:T(8,128)}) custom-call(f32[128]{0:T(128)} %constant.10.clone.shift_ref.refs_0_, f32[4,128]{1,0:T(4,128)} %refs_1_.1, s32[8,128]{1,0:T(8,128)} %get-tuple-element.9.refs_2_, bf16[264,96]{1,0:T(8,128)(2,1)} %constant.11.clone.refs_3_, bf16[264,96]{1,0:T(8,128)(2,1)} %constant.12.clone.refs_4_, ...), custom_call_target="tpu_custom_call" | custom-call | tf_op jit(solution)/shard_map/pallas_call | solution.py:771

commit v4 on v3

--- a/solution.py
+++ b/solution.py
@@ -442,12 +442,12 @@
             device_id_type=MESH,
         )
 
-    def returning(half, k):
+    def returning(half, f, k):
         return pltpu.make_async_remote_copy(
-            src_ref=back_send.at[half, peers[k]],
-            dst_ref=back_recv.at[half, me],
-            send_sem=back_send_sem.at[half, k],
-            recv_sem=back_recv_sem.at[half, k],
+            src_ref=back_send.at[half, peers[k], pl.ds(88 * f, 88)],
+            dst_ref=back_recv.at[half, me, pl.ds(88 * f, 88)],
+            send_sem=back_send_sem.at[half, f, k],
+            recv_sem=back_recv_sem.at[half, f, k],
             device_id=(row, peers[k]),
             device_id_type=MESH,
         )
@@ -571,20 +571,22 @@
             return carry
 
         lax.fori_loop(0, 8, collect, 0, unroll=2)
-        for k in range(1, 8):
-            returning(half, k).start()
+        for f in range(3):
+            for k in range(1, 8):
+                returning(half, f, k).start()
         back_recv[half, me] = back_send[half, me]
 
     sweep(1)
     sweep(2)
 
-    for half in range(2):
-        for k in range(1, 8):
-            returning(half, k).wait_recv()
     fa, _, fc = factor_rows(metrics_ref)
     base = spectral_bound * (fa + fc) + penalty_weight
+    second_halo = []
     for f in range(3):
         advection, kept, state = Field(adv_ref, f), Field(part_ref, f), Field(state_ref, f)
+        for half in range(2):
+            for k in range(1, 8):
+                returning(half, f, k).wait_recv()
         for tile in range(11):
             first = 88 * f + 8 * tile
             planes = swap_groups(
@@ -598,14 +600,17 @@
                 value = kept.tile(c, tile) - weight * advection.tile(c, tile)
                 state.put(c, tile, value)
         emit_halo(state, table_ref, down2_ref, up2_ref, f, fields)
-    second_halo = halo_copies(1, down2_ref, up2_ref, low2_ref, top2_ref)
-    for copy in second_halo:
-        copy.start()
+        copies = halo_copies(
+            1 + f, down2_ref.at[f], up2_ref.at[f], low2_ref.at[f], top2_ref.at[f]
+        )
+        for copy in copies:
+            copy.start()
+        second_halo.extend(copies)
     for half in range(2):
         for k in range(1, 8):
             for f in range(3):
                 outgoing(half, f, k).wait_send()
-            returning(half, k).wait_send()
+                returning(half, f, k).wait_send()
     for copy in second_halo:
         copy.wait()
 
@@ -712,9 +717,8 @@
             + [pltpu.VMEM((1024, LANES), jnp.float32)] * 6
             + [pltpu.VMEM(velocity.shape, jnp.float32)]
             + [halo_buffer] * 6
-            + [pltpu.SemaphoreType.DMA((2, 3, 8))] * 2
-            + [pltpu.SemaphoreType.DMA((2, 8))] * 2
-            + [pltpu.SemaphoreType.DMA((2, 2))] * 2
+            + [pltpu.SemaphoreType.DMA((2, 3, 8))] * 4
+            + [pltpu.SemaphoreType.DMA((4, 2))] * 2
             + [pltpu.SemaphoreType.DMA((9,))],
             compiler_params=pltpu.CompilerParams(
                 vmem_limit_bytes=60 << 20, collective_id=0, has_side_effects=True

time: 80.9 us -> 75.6 us (0.934)
  Pallas kernels: 80.1 us -> 74.2 us
    pallas_call x1, Pallas kernels: 70.7 us -> 64.9 us  [body(): pl.pallas_call(functools.partial(fused_kernel, lax.axis_size('mesh')), in...]
where the time goes in v4:
time: 75.6 us; the launch traced here: 74.9 us
  Pallas kernels  74.2 us (98%)
    pallas_call x1, Pallas kernels, body(): pl.pallas_call(functools.partial(fused_kernel, lax.axis_size('mesh')), in...  64.9 us
    pallas_call x1, Pallas kernels, body(): pl.pallas_call(functools.partial(last_kernel, fields), grid=(3,), in_spec...  9.37 us

profile of v4, /device:TPU:1, one launch (start us, length us, event | category | flops | bytes accessed | tf_op | source)
XLA Modules:
  0.0 74.9 jit_solution(17830997744341535442)
XLA Ops:
  0.6 64.9 %shard_map.113 = (f32[3,16,81,128]{3,2,1,0:T(8,128)}, f32[3,16,81,128]{3,2,1,0:T(8,128)}, f32[3,72,128]{2,1,0:T(8,128)}, f32[3,72,128]{2,1,0:T(8,128)}, s32[8,128]{1,0:T(8,128)}) custom-call(f32[128]{0:T(128)} %constant.10.clone.shift_ref.refs_0_, f32[4,128]{1,0:T(4,128)} %refs_1_.1, f32[4,128]{1,0:T(4,128)} %refs_1_.1, s32[4,128]{1,0:T(4,128)} %bitcast.13, ...), custom_call_target="tpu_custom_call" | custom-call | tf_op jit(solution)/shard_map/pallas_call | solution.py:696
  65.5 9.4 %shard_map.114 = (f32[3,1296,128]{2,1,0:T(8,128)}, f32[3,1296,128]{2,1,0:T(8,128)}) custom-call(f32[128]{0:T(128)} %constant.10.clone.shift_ref.refs_0_, f32[4,128]{1,0:T(4,128)} %refs_1_.1, s32[8,128]{1,0:T(8,128)} %get-tuple-element.9.refs_2_, bf16[264,96]{1,0:T(8,128)(2,1)} %constant.11.clone.refs_3_, bf16[264,96]{1,0:T(8,128)(2,1)} %constant.12.clone.refs_4_, ...), custom_call_target="tpu_custom_call" | custom-call | tf_op jit(solution)/shard_map/pallas_call | solution.py:775
